TPU v7x, 256 devices: a whole 4x4x8 slice. The times are simulated.
256 devices in a mesh: pipe: 8 (over y, core), dp: 32 (over z, x).
Axes of the slice: x: 4, y: 4, z: 8, core: 2. Of those that a mesh axis runs over, the one named last changes fastest.
Arguments:
- queries: bfloat16 [8, 7680, 4096], P('pipe', 'dp'), may hold values from -8 to 8
- out_grad: bfloat16 [8, 7680, 4096], P('pipe', 'dp'), may hold values from -16 to 16
- key_weight: bfloat16 [8, 512, 4096], P('pipe', 'dp'), may hold values from -0.25 to 0.25
- value_weight: bfloat16 [8, 512, 4096], P('pipe', 'dp'), may hold values from -0.25 to 0.25
- encoded: bfloat16 [8, 64, 128, 512], P('pipe', 'dp'), may hold values from -4 to 4
- nb_owner: int32 [8, 192, 2], P('pipe', 'dp'), may hold values from 0 to 31, as said below
- nb_block: int32 [8, 192, 2], P('pipe', 'dp'), may hold values from 0 to 1
Outputs:
- query_grad: bfloat16 [8, 7680, 4096], P('pipe', 'dp')
- encoded_grad: float32 [8, 64, 128, 512], P('pipe', 'dp')
Inputs may be any that keep to these rules, and one draw needn't show every extreme that they name: `nb_owner`: the 12 entries of one group of 6 consecutive spans name exactly 11 different owners; two entries of one group that name the same owner name the same block.
All inputs are finite; a program needn't handle non-finite values.
Results may differ from a plain program's by a relative error of at most 0.014.
Values may be sent and summed in bfloat16 or wider, within the bound.
No kernel may reach another device: no remote copies, remote signals or barrier semaphores. Data moves between devices by JAX's collectives and lax.ppermute only.
A program may use at most 128 MiB of HBM per device.

v0:
```python
import functools
import jax
import jax.numpy as jnp
from jax import lax
from jax.experimental import pallas as pl
from jax.experimental.pallas import tpu as pltpu
from jax.sharding import PartitionSpec as P

SPAN = 40
HEAD_DIM = 128
SCALE = HEAD_DIM ** (-0.5)
NX = 4
F32 = jnp.float32
BF16 = jnp.bfloat16


def dot(a, b, ca, cb):
    return lax.dot_general(a, b, (((ca,), (cb,)), ((), ())), preferred_element_type=F32)


def weight_copies(here, ring, dest, sems):
    nz = len(ring) - 1
    copies = []
    for i, piece in enumerate(ring):
        away = (i + 1) // 2 if i < nz else nz // 2
        away = away if i % 2 else nz - away
        row = here + nz - away
        row = jnp.where(row >= 2 * nz, row - 2 * nz, jnp.where(row >= nz, row - nz, row))
        count = piece.shape[0]
        start = row * NX + (NX - count if i == nz else 0)
        copies.append(pltpu.make_async_copy(piece, dest.at[pl.ds(start, count)], sems.at[i]))
    return copies


def key_copies(slot_ref, arrived, dest, sems):
    rows = arrived.shape[1]
    per = dest.shape[1] // rows
    return [
        pltpu.make_async_copy(
            arrived.at[slot_ref[e]], dest.at[e // per, pl.ds(e % per * rows, rows)], sems.at[e]
        )
        for e in range(slot_ref.shape[0])
    ]


def head_weight(block, h):
    ranks, _, width = block.shape
    per = width // HEAD_DIM
    rows = 16
    part = block[:, h // per * rows : (h // per + 1) * rows, h % per * HEAD_DIM : (h % per + 1) * HEAD_DIM]
    return part.reshape(ranks * rows, HEAD_DIM)


def grads_kernel(heads, pieces, slot_ref, here_ref, row_slot, dense_slot, first_ref, q_ref, g_ref, arrived, *refs):
    key_ring, value_ring = refs[:pieces], refs[pieces : 2 * pieces]
    ds_ref, row_ref, dense_ref = refs[2 * pieces : 2 * pieces + 3]
    key_w, value_w, keys_ref, a_ref, b_ref, sum_ref, sem_k, sem_v, sem_e = refs[2 * pieces + 3 :]
    step = pl.program_id(0)
    here = here_ref[0]
    of_keys = weight_copies(here, key_ring, key_w, sem_k)
    of_values = weight_copies(here, value_ring, value_w, sem_v)
    of_rows = key_copies(slot_ref, arrived, keys_ref, sem_e)

    @pl.when(step == 0)
    def _():
        for copy in of_keys + of_values + of_rows:
            copy.start()

        @pl.loop(0, row_ref.shape[0])
        def _(n):
            row_ref[n] = jnp.zeros(row_ref.shape[1:], BF16)
            dense_ref[n] = jnp.zeros(row_ref.shape[1:], BF16)

    spans = a_ref.shape[0]
    quad = key_w.shape[2] // HEAD_DIM
    for src, weight, out, copies in (
        (q_ref, key_w, a_ref, of_keys),
        (g_ref, value_w, b_ref, of_values),
    ):

        @pl.when(step == 0)
        def _():
            for copy in copies:
                copy.wait()

        @pl.loop(0, heads // quad)
        def _(q):
            block = weight[:, pl.ds(pl.multiple_of((step * (heads // quad) + q) * 16, 16), 16), :]
            source = src[:, pl.ds(pl.multiple_of(q * quad * HEAD_DIM, quad * HEAD_DIM), quad * HEAD_DIM)]
            for pair in range(quad // 2):
                wide = []
                for h in (2 * pair, 2 * pair + 1):
                    wide.append(dot(source[:, h * HEAD_DIM : (h + 1) * HEAD_DIM], head_weight(block, h), 1, 1))
                rows = pl.ds(pl.multiple_of((q * quad + 2 * pair) * SPAN, 16), 2 * SPAN)
                for a in range(spans):
                    part = slice(a * SPAN, (a + 1) * SPAN)
                    both = jnp.concatenate([wide[0][part], wide[1][part]], axis=0)
                    out[a, rows, :] = both.astype(BF16)

    @pl.when(step == 0)
    def _():
        for copy in of_rows:
            copy.wait()

    @pl.loop(0, spans)
    def _(a):
        keys = keys_ref[a]
        e = jnp.exp(SCALE * dot(keys, a_ref[a], 1, 1))
        total = jnp.sum(e, axis=0, keepdims=True)
        guard = jnp.where(total > 1e30, 2.0**-24, 1.0)
        probs = (e * guard) * (1.0 / (total * guard))
        grad = dot(keys, b_ref[a], 1, 1)
        delta = jnp.sum(probs * grad, axis=0, keepdims=True)
        ds = (probs * (grad - delta)).astype(BF16)
        ds_ref[a] = ds
        entry = SCALE * dot(ds, a_ref[a], 1, 0) + dot(probs.astype(BF16), b_ref[a], 1, 0)

        @pl.when(step == 0)
        def _():
            sum_ref[a] = entry

        @pl.when(step > 0)
        def _():
            sum_ref[a] = sum_ref[a] + entry

    @pl.when(step == pl.num_programs(0) - 1)
    def _():
        length = row_ref.shape[1]
        half = row_ref.shape[2]
        per = sum_ref.shape[1] // length

        def rows_of(n):
            span = n // per
            return span, pl.ds(pl.multiple_of((n - span * per) * length, length), length)

        @pl.loop(0, slot_ref.shape[0])
        def _(n):
            first = first_ref[n]

            @pl.when(first != n)
            def _():
                sum_ref[rows_of(first)] = sum_ref[rows_of(first)] + sum_ref[rows_of(n)]

        @pl.loop(0, slot_ref.shape[0])
        def _(n):
            @pl.when(first_ref[n] == n)
            def _():
                value = sum_ref[rows_of(n)].astype(BF16)
                row_ref[row_slot[n]] = value[:, :half]
                dense_ref[dense_slot[n]] = value[:, half:]


def grads_call(slots, here, row_slot, dense_slot, first, q, g, arrived, key_ring, value_ring, spans, groups):
    tok, hd = q.shape
    ranks, rows, enc = arrived.shape
    entries = slots.shape[0]
    kr = entries // spans * rows
    heads = hd // HEAD_DIM // groups
    m = heads * SPAN
    cols = heads * HEAD_DIM
    pieces = len(key_ring)
    wide = (ranks,) + key_ring[0].shape[1:]
    anywhere = pl.BlockSpec(memory_space=pl.ANY)
    whole = pl.BlockSpec((ranks, rows, enc // 2), lambda i, *_: (0, 0, 0))
    return pl.pallas_call(
        functools.partial(grads_kernel, heads, pieces),
        grid_spec=pltpu.PrefetchScalarGridSpec(
            num_scalar_prefetch=5,
            grid=(groups,),
            in_specs=[
                pl.BlockSpec((tok, cols), lambda i, *_: (0, i)),
                pl.BlockSpec((tok, cols), lambda i, *_: (0, i)),
            ]
            + [anywhere] * (1 + 2 * pieces),
            out_specs=[pl.BlockSpec((spans, kr, m), lambda i, *_: (0, 0, i)), whole, whole],
            scratch_shapes=[
                pltpu.VMEM(wide, BF16),
                pltpu.VMEM(wide, BF16),
                pltpu.VMEM((spans, kr, enc), BF16),
                pltpu.VMEM((spans, m, enc), BF16),
                pltpu.VMEM((spans, m, enc), BF16),
                pltpu.VMEM((spans, kr, enc), F32),
                pltpu.SemaphoreType.DMA((pieces,)),
                pltpu.SemaphoreType.DMA((pieces,)),
                pltpu.SemaphoreType.DMA((entries,)),
            ],
        ),
        out_shape=[
            jax.ShapeDtypeStruct((spans, kr, m * groups), BF16),
            jax.ShapeDtypeStruct((ranks, rows, enc // 2), BF16),
            jax.ShapeDtypeStruct((ranks, rows, enc // 2), BF16),
        ],
        name="grads",
        cost_estimate=pl.CostEstimate(flops=10**10, bytes_accessed=25 * 10**6, transcendentals=2 * 10**6),
        compiler_params=pltpu.CompilerParams(vmem_limit_bytes=56 << 20),
    )(slots, here, row_slot, dense_slot, first, q, g, arrived, *key_ring, *value_ring)


def query_kernel(heads, pieces, slot_ref, here_ref, ds_ref, arrived, *refs):
    key_ring = refs[:pieces]
    o_ref, wide_ref, key_w, keys_ref, sem_k, sem_e = refs[pieces:]
    step = pl.program_id(0)

    @pl.when(step == 0)
    def _():
        copies = weight_copies(here_ref[0], key_ring, key_w, sem_k) + key_copies(
            slot_ref, arrived, keys_ref, sem_e
        )
        for copy in copies:
            copy.start()
        for copy in copies:
            copy.wait()

    spans = ds_ref.shape[0]
    quad = key_w.shape[2] // HEAD_DIM

    @pl.loop(0, spans)
    def _(a):
        wide = SCALE * dot(ds_ref[a], keys_ref[a], 0, 0)
        for h in range(heads):
            wide_ref[h, pl.ds(pl.multiple_of(a * SPAN, 8), SPAN), :] = wide[h * SPAN : (h + 1) * SPAN]

    @pl.loop(0, heads // quad)
    def _(q):
        block = key_w[:, pl.ds(pl.multiple_of((step * (heads // quad) + q) * 16, 16), 16), :]
        parts = [
            dot(wide_ref[q * quad + h].astype(BF16), head_weight(block, h), 1, 0).astype(BF16)
            for h in range(quad)
        ]
        width = quad * HEAD_DIM
        o_ref[:, pl.ds(pl.multiple_of(q * width, width), width)] = jnp.concatenate(parts, axis=1)


def query_call(slots, here, ds, arrived, key_ring, groups):
    spans, kr, m_all = ds.shape
    ranks, _, enc = arrived.shape
    entries = slots.shape[0]
    m = m_all // groups
    heads = m // SPAN
    cols = heads * HEAD_DIM
    tok = spans * SPAN
    pieces = len(key_ring)
    anywhere = pl.BlockSpec(memory_space=pl.ANY)
    return pl.pallas_call(
        functools.partial(query_kernel, heads, pieces),
        grid_spec=pltpu.PrefetchScalarGridSpec(
            num_scalar_prefetch=2,
            grid=(groups,),
            in_specs=[pl.BlockSpec((spans, kr, m), lambda i, *_: (0, 0, i))] + [anywhere] * (1 + pieces),
            out_specs=pl.BlockSpec((tok, cols), lambda i, *_: (0, i)),
            scratch_shapes=[
                pltpu.VMEM((heads, tok, enc), F32),
                pltpu.VMEM((ranks,) + key_ring[0].shape[1:], BF16),
                pltpu.VMEM((spans, kr, enc), BF16),
                pltpu.SemaphoreType.DMA((pieces,)),
                pltpu.SemaphoreType.DMA((entries,)),
            ],
        ),
        out_shape=jax.ShapeDtypeStruct((tok, cols * groups), BF16),
        name="query_grad",
        cost_estimate=pl.CostEstimate(flops=3 * 10**9, bytes_accessed=12 * 10**6, transcendentals=0),
        compiler_params=pltpu.CompilerParams(vmem_limit_bytes=56 << 20),
    )(slots, here, ds, arrived, *key_ring)


def serve_kernel(table_ref, *refs):
    sources, (out_ref, sem) = refs[:-2], refs[-2:]
    steps = len(sources)
    here = table_ref[out_ref.shape[0]]
    copies = []
    for slot in range(out_ref.shape[0]):
        back = slot % steps
        row = jnp.where(here >= back, here - back, here - back + steps)
        block = jnp.maximum(table_ref[slot // steps * steps + row], 0)
        copies.append(pltpu.make_async_copy(sources[back].at[block], out_ref.at[slot], sem.at[slot]))
        copies[-1].start()
    for copy in copies:
        copy.wait()


def serve_call(table, sources):
    _, rows, enc = sources[0].shape
    slots = table.shape[0] - 1
    return pl.pallas_call(
        serve_kernel,
        in_specs=[pl.BlockSpec(memory_space=pltpu.SMEM)]
        + [pl.BlockSpec(memory_space=pl.ANY)] * len(sources),
        out_specs=pl.BlockSpec(memory_space=pltpu.VMEM),
        out_shape=jax.ShapeDtypeStruct((slots, rows, enc), BF16),
        scratch_shapes=[pltpu.SemaphoreType.DMA((slots,))],
        name="serve",
        cost_estimate=pl.CostEstimate(flops=0, bytes_accessed=8 * 10**6, transcendentals=0),
    )(table, *sources)


def pairs_x(groups, shift):
    return [(d, d // NX * NX + (d % NX + shift) % NX) for d in range(groups)]


def pairs_z(groups, shift):
    return [(d, (d + shift * NX) % groups) for d in range(groups)]


def tied(value, *others):
    return lax.optimization_barrier((value,) + others)[0]


def shards(queries, out_grad, key_weight, value_weight, encoded, nb_owner, nb_block):
    groups = lax.axis_size("dp")
    nz = groups // NX
    pipe = lax.axis_size("pipe")
    held, rows, enc = encoded.shape[1:]
    owners = nb_owner[0].reshape(-1)
    blocks = nb_block[0].reshape(-1)
    spans = nb_owner.shape[1]
    here, side = lax.axis_index("dp") // NX, lax.axis_index("dp") % NX
    over_x = [[z * NX + x for x in range(NX)] for z in range(nz)]

    def exchange(v, among=None):
        return lax.all_to_all(v, "dp", split_axis=0, concat_axis=0, tiled=True, axis_index_groups=among)

    def send_x(v, shift):
        return lax.ppermute(v, "dp", pairs_x(groups, shift))

    def send_z(v, shift):
        return lax.ppermute(v, "dp", pairs_z(groups, shift))

    def ring_move(ring):
        up, down = ring[-2:] if len(ring) > 1 else ring * 2
        if len(ring) == nz - 1:
            half = up.shape[0] // 2
            up, down = up[:half], down[half:]
        return ring + [send_z(up, 1), send_z(down, -1)]

    def pieces_of(weight):
        _, rows, _ = weight.shape
        cols = 4 * HEAD_DIM
        return weight.reshape(rows, -1, cols).swapaxes(0, 1).reshape(-1, cols)

    mine = jnp.stack([pieces_of(key_weight), pieces_of(value_weight)])
    row_weights = exchange(jnp.broadcast_to(mine[None], (NX,) + mine.shape), over_x)
    held_rows = ring_move([encoded[0]])
    held_rows[1:] = lax.optimization_barrier((held_rows[1], held_rows[2], row_weights))[:2]

    column_major = owners % NX * nz + owners // NX
    slot_ids = jnp.arange(groups, dtype=jnp.int32)[:, None]
    request = jnp.max(jnp.where(column_major[None, :] == slot_ids, blocks[None, :], -1), axis=1)
    by_column = jnp.broadcast_to(request.reshape(1, NX, nz), (nz, NX, nz)).reshape(groups, nz)
    asked = exchange(tied(by_column, row_weights))
    wanted = lax.dynamic_slice_in_dim(asked, here, 1, axis=1)[:, 0]
    row_wanted = lax.dynamic_slice_in_dim(asked, here * NX, NX, axis=0)

    keys, values = [row_weights[:, 0]], [row_weights[:, 1]]
    for _ in range(nz // 2 - 1):
        held_rows = ring_move(held_rows)
    for _ in range(nz // 2):
        keys, values = ring_move(keys), ring_move(values)
    far = jnp.concatenate(held_rows[-2:])
    in_order = held_rows[:1] + held_rows[1 : nz - 1 : 2] + [far] + held_rows[nz - 2 : 0 : -2]
    table = jnp.concatenate([row_wanted.reshape(-1), here[None]]).astype(jnp.int32)
    served = serve_call(table, in_order)
    arrived = exchange(served, over_x)
    incoming = lax.ppermute(out_grad, "pipe", [(s, (s - 1) % pipe) for s in range(pipe)])[0]

    slots = (owners % NX * nz + (here - owners // NX) % nz).astype(jnp.int32)
    hop_x, hop_z = (owners % NX - side) % NX, (owners // NX - here) % nz
    row_slot = (hop_x * nz + hop_z).astype(jnp.int32)
    first = jnp.argmax(owners[:, None] == owners[None, :], axis=1).astype(jnp.int32)
    by_side = jnp.take(row_wanted, (side - jnp.arange(NX)) % NX, axis=0)
    row_blocks = jnp.take(by_side, (here + jnp.arange(nz)) % nz, axis=1)
    at = here[None].astype(jnp.int32)
    slots, first, row_slot, wanted, row_blocks = lax.optimization_barrier(
        (slots, first, row_slot, wanted, row_blocks)
    )

    ds, part, dense = grads_call(
        slots, at, row_slot, owners, first, queries[0], incoming, arrived, keys, values, spans, 2
    )
    returned = exchange(dense)
    pieces = [part[:nz]]
    for shift in range(1, NX):
        pieces.append(send_x(part[shift * nz : (shift + 1) * nz], shift))
    query_grad = query_call(slots, at, ds, arrived, keys, 2)

    held_ids = jnp.arange(held, dtype=jnp.int32)
    row_sum = [jnp.zeros((nz, rows, enc // 2), F32)] * held
    for piece, of_piece in zip(pieces, row_blocks):
        for block in range(held):
            chosen = (of_piece == block).astype(F32)[:, None, None]
            row_sum[block] = row_sum[block] + chosen * piece.astype(F32)
    row_sum = jnp.stack(row_sum, axis=1).astype(BF16)
    left = row_sum[0].astype(F32)
    for shift in range(1, nz):
        left = left + send_z(row_sum[shift], shift).astype(F32)
    choose = (wanted[:, None] == held_ids[None, :]).astype(BF16)
    right = jnp.dot(choose.T, returned.reshape(groups, -1), preferred_element_type=F32)
    encoded_grad = jnp.concatenate([left, right.reshape(left.shape)], axis=-1)
    return query_grad[None], encoded_grad[None]


def solution(mesh):
    cut = P("pipe", "dp", None)
    deep = P("pipe", "dp", None, None)

    return jax.shard_map(
        shards,
        mesh=mesh,
        in_specs=(cut, cut, cut, cut, deep, cut, cut),
        out_specs=(cut, deep),
        check_vma=False,
    )
```

profile of v0, /device:TPU:22, one launch (start us, length us, event | category | flops | bytes accessed | tf_op | source)
XLA Modules:
  0.0 264.3 jit_solution(8306443302337919504)
XLA Ops:
  1.6 0.9 copy.79
  2.7 1.1 broadcast_in_dim.72
  3.8 4.8 %all-to-all-start = ((bf16[4,2,128,512]{3,2,1,0:T(8,128)(2,1)}), bf16[4,2,128,512]{3,2,1,0:T(8,128)(2,1)S(1)}, u32[]{:S(2)}, u32[]{:S(2)}) async-start(bf16[4,2,128,512]{3,2,1,0:T(8,128)(2,1)} %broadcast_in_dim.72), calls=%async_computation | async-start | bytes 2097152 | tf_op jit(solution)/shard_map/all_to_all | solution.py:320
  8.5 5.9 %collective-permute-start.2 = (bf16[2,128,512]{2,1,0:T(8,128)(2,1)S(1)}, bf16[2,128,512]{2,1,0:T(8,128)(2,1)S(1)}, u32[]{:S(2)}, u32[]{:S(2)}) collective-permute-start(bf16[2,128,512]{2,1,0:T(8,128)(2,1)S(1)} %bitcast.92), channel_id=1, source_target_pairs={{0,28},{1,29},{2,30},{3,31},{4,0},{5,1},{6,2},{7,3},{8,4},{9,5},{1... | collective-permute-start | bytes 786440 | tf_op jit(solution)/shard_map/ppermute | solution.py:326
  14.4 5.0 %collective-permute-done.2.refs_7_ = bf16[2,128,512]{2,1,0:T(8,128)(2,1)S(1)} collective-permute-done((bf16[2,128,512]{2,1,0:T(8,128)(2,1)S(1)}, bf16[2,128,512]{2,1,0:T(8,128)(2,1)S(1)}, u32[]{:S(2)}, u32[]{:S(2)}) %collective-permute-start.2) | collective-permute-done | bytes 262176 | tf_op jit(solution)/shard_map/ppermute | solution.py:326
  19.4 3.4 %collective-permute-done.1.refs_1_ = bf16[2,128,512]{2,1,0:T(8,128)(2,1)S(1)} collective-permute-done((bf16[2,128,512]{2,1,0:T(8,128)(2,1)S(1)}, bf16[2,128,512]{2,1,0:T(8,128)(2,1)S(1)}, u32[]{:S(2)}, u32[]{:S(2)}) %collective-permute-start.1) | collective-permute-done | bytes 262176 | tf_op jit(solution)/shard_map/ppermute | solution.py:326
  23.5 3.9 %collective-permute-start.6 = (bf16[2,128,512]{2,1,0:T(8,128)(2,1)S(1)}, bf16[2,128,512]{2,1,0:T(8,128)(2,1)S(1)}, u32[]{:S(2)}, u32[]{:S(2)}) collective-permute-start(bf16[2,128,512]{2,1,0:T(8,128)(2,1)S(1)} %collective-permute-done.2.refs_7_), channel_id=1, source_target_pairs={{0,28},{1,29},{2,30},{3,31},{4,0},{5,1},{6,2},{7,3},{8,4},{9,5},{1... | collective-permute-start | bytes 786440 | tf_op jit(solution)/shard_map/ppermute | solution.py:326
  27.8 4.8 %collective-permute-done.3.refs_2_ = bf16[2,128,512]{2,1,0:T(8,128)(2,1)S(1)} collective-permute-done((bf16[2,128,512]{2,1,0:T(8,128)(2,1)S(1)}, bf16[2,128,512]{2,1,0:T(8,128)(2,1)S(1)}, u32[]{:S(2)}, u32[]{:S(2)}) %collective-permute-start.3) | collective-permute-done | bytes 262176 | tf_op jit(solution)/shard_map/ppermute | solution.py:326
  32.6 3.2 %collective-permute-start.7 = (bf16[2,128,512]{2,1,0:T(8,128)(2,1)S(1)}, bf16[2,128,512]{2,1,0:T(8,128)(2,1)S(1)}, u32[]{:S(2)}, u32[]{:S(2)}) collective-permute-start(bf16[2,128,512]{2,1,0:T(8,128)(2,1)S(1)} %collective-permute-done.6.refs_6_), channel_id=1, source_target_pairs={{0,28},{1,29},{2,30},{3,31},{4,0},{5,1},{6,2},{7,3},{8,4},{9,5},{1... | collective-permute-start | bytes 786440 | tf_op jit(solution)/shard_map/ppermute | solution.py:326
  36.6 8.4 %all-to-all-start.1 = ((s32[32,1,8]{2,1,0:T(1,128)}), s32[32,1,8]{2,1,0:T(1,128)S(1)}, u32[]{:S(2)}, u32[]{:S(2)}) async-start(s32[32,1,8]{2,1,0:T(1,128)} %bitcast.5), calls=%async_computation.1 | async-start | bytes 32768 | tf_op jit(solution)/shard_map/all_to_all | solution.py:320
  45.1 1.5 collective-permute-start.5
  46.6 1.8 collective-permute-start.8
  48.5 4.7 %all-to-all-done.1 = s32[32,1,8]{2,1,0:T(1,128)S(1)} async-done(((s32[32,1,8]{2,1,0:T(1,128)}), s32[32,1,8]{2,1,0:T(1,128)S(1)}, u32[]{:S(2)}, u32[]{:S(2)}) %all-to-all-start.1) | async-done | bytes 1056 | tf_op jit(solution)/shard_map/all_to_all | solution.py:320
  55.9 5.5 %serve.1 = bf16[32,128,512]{2,1,0:T(8,128)(2,1)} custom-call(s32[33]{0:T(128)} %pad_add_fusion.table_ref, bf16[2,128,512]{2,1,0:T(8,128)(2,1)} %bitcast.91, bf16[2,128,512]{2,1,0:T(8,128)(2,1)} %copy-done.12, bf16[2,128,512]{2,1,0:T(8,128)(2,1)} %copy-done.13, bf16[2,128,512]{2,1,0:T(8,128)(2,1)} %copy-done.3, ...), custom_call_target="tpu_custom_call" | custom-call | bytes 8000000 | tf_op jit(solution)/shard_map/serve/pallas_call | solution.py:284
  61.3 6.7 %all-to-all-start.2 = ((bf16[32,128,512]{2,1,0:T(8,128)(2,1)}), bf16[32,128,512]{2,1,0:T(8,128)(2,1)}, u32[]{:S(2)}, u32[]{:S(2)}) async-start(bf16[32,128,512]{2,1,0:T(8,128)(2,1)} %serve.1), calls=%async_computation.2 | async-start | bytes 8388608 | tf_op jit(solution)/shard_map/all_to_all | solution.py:320
  69.1 1.2 collective-permute-start.17
  70.3 2.1 collective-permute-start.10
  72.4 10.7 %collective-permute-done.18.refs_11_ = bf16[4,128,512]{2,1,0:T(8,128)(2,1)S(1)} collective-permute-done((bf16[4,128,512]{2,1,0:T(8,128)(2,1)S(1)}, bf16[4,128,512]{2,1,0:T(8,128)(2,1)S(1)}, u32[]{:S(2)}, u32[]{:S(2)}) %collective-permute-start.18) | collective-permute-done | bytes 524320 | tf_op jit(solution)/shard_map/ppermute | solution.py:326
  83.1 2.1 collective-permute-start.20
  85.1 9.1 %collective-permute-done.10.refs_2_ = bf16[4,128,512]{2,1,0:T(8,128)(2,1)S(1)} collective-permute-done((bf16[4,128,512]{2,1,0:T(8,128)(2,1)S(1)}, bf16[4,128,512]{2,1,0:T(8,128)(2,1)S(1)}, u32[]{:S(2)}, u32[]{:S(2)}) %collective-permute-start.10) | collective-permute-done | bytes 524320 | tf_op jit(solution)/shard_map/ppermute | solution.py:326
  94.3 2.1 collective-permute-start.12
  96.4 9.2 %collective-permute-done.20.refs_13_ = bf16[4,128,512]{2,1,0:T(8,128)(2,1)} collective-permute-done((bf16[4,128,512]{2,1,0:T(8,128)(2,1)S(1)}, bf16[4,128,512]{2,1,0:T(8,128)(2,1)}, u32[]{:S(2)}, u32[]{:S(2)}) %collective-permute-start.20) | collective-permute-done | bytes 524320 | tf_op jit(solution)/shard_map/ppermute | solution.py:326
  105.6 2.1 collective-permute-start.22
  107.7 9.1 %collective-permute-done.12.refs_4_ = bf16[4,128,512]{2,1,0:T(8,128)(2,1)S(1)} collective-permute-done((bf16[4,128,512]{2,1,0:T(8,128)(2,1)S(1)}, bf16[4,128,512]{2,1,0:T(8,128)(2,1)S(1)}, u32[]{:S(2)}, u32[]{:S(2)}) %collective-permute-start.12) | collective-permute-done | bytes 524320 | tf_op jit(solution)/shard_map/ppermute | solution.py:326
  116.8 2.1 collective-permute-start.14
  120.8 7.3 %collective-permute-done.22.refs_15_ = bf16[4,128,512]{2,1,0:T(8,128)(2,1)} collective-permute-done((bf16[4,128,512]{2,1,0:T(8,128)(2,1)}, bf16[4,128,512]{2,1,0:T(8,128)(2,1)}, u32[]{:S(2)}, u32[]{:S(2)}) %collective-permute-start.22) | collective-permute-done | bytes 524320 | tf_op jit(solution)/shard_map/ppermute | solution.py:326
  128.1 1.7 slice.91
  129.8 2.1 collective-permute-start.24
  131.9 1.7 slice.90
  133.6 5.7 %collective-permute-done.14.refs_6_ = bf16[4,128,512]{2,1,0:T(8,128)(2,1)S(1)} collective-permute-done((bf16[4,128,512]{2,1,0:T(8,128)(2,1)S(1)}, bf16[4,128,512]{2,1,0:T(8,128)(2,1)S(1)}, u32[]{:S(2)}, u32[]{:S(2)}) %collective-permute-start.14) | collective-permute-done | bytes 524320 | tf_op jit(solution)/shard_map/ppermute | solution.py:326
  140.0 2.0 collective-permute-start.16
  144.4 2.2 collective-permute-done.16.refs_8_
  146.6 4.1 %collective-permute-done.15.refs_7_ = bf16[2,128,512]{2,1,0:T(8,128)(2,1)} collective-permute-done((bf16[2,128,512]{2,1,0:T(8,128)(2,1)}, bf16[2,128,512]{2,1,0:T(8,128)(2,1)}, u32[]{:S(2)}, u32[]{:S(2)}) %collective-permute-start.15) | collective-permute-done | bytes 262176 | tf_op jit(solution)/shard_map/ppermute | solution.py:326
  150.7 30.6 %grads.1 = (bf16[6,256,1280]{2,1,0:T(8,128)(2,1)}, bf16[32,128,256]{2,1,0:T(8,128)(2,1)}, bf16[32,128,256]{2,1,0:T(8,128)(2,1)}) custom-call(s32[12]{0:T(128)} %get-tuple-element.16.slot_ref, s32[1]{0:T(128)} %bitcast.10.here_ref, s32[12]{0:T(128)} %get-tuple-element.17.row_slot, s32[12]{0:T(128)} %copy-done.15, s32[12]{0:T(128)} %get-tuple-element.18.first_ref, ...), custom_call_target="tpu_custom_call" | custom-call | flops 10000000000 | bytes 25000000 | tf_op jit(solution)/shard_map/grads/pallas_call | solution.py:165
  181.3 7.2 %all-to-all-start.3 = ((bf16[32,128,256]{2,1,0:T(8,128)(2,1)}), bf16[32,128,256]{2,1,0:T(8,128)(2,1)S(1)}, u32[]{:S(2)}, u32[]{:S(2)}) async-start(bf16[32,128,256]{2,1,0:T(8,128)(2,1)} %get-tuple-element.25), calls=%async_computation.3 | async-start | bytes 4194304 | tf_op jit(solution)/shard_map/all_to_all | solution.py:320
  188.5 1.5 fusion.50
  190.3 1.8 collective-permute-start.27
  192.1 1.5 collective-permute-start.26
  193.8 22.0 %collective-permute-done.25 = bf16[8,128,256]{2,1,0:T(8,128)(2,1)S(1)} collective-permute-done((bf16[8,128,256]{2,1,0:T(8,128)(2,1)S(1)}, bf16[8,128,256]{2,1,0:T(8,128)(2,1)S(1)}, u32[]{:S(2)}, u32[]{:S(2)}) %collective-permute-start.25) | collective-permute-done | bytes 524320 | tf_op jit(solution)/shard_map/ppermute | solution.py:323
  215.8 13.0 %collective-permute-done.26 = bf16[8,128,256]{2,1,0:T(8,128)(2,1)S(1)} collective-permute-done((bf16[8,128,256]{2,1,0:T(8,128)(2,1)S(1)}, bf16[8,128,256]{2,1,0:T(8,128)(2,1)S(1)}, u32[]{:S(2)}, u32[]{:S(2)}) %collective-permute-start.26) | collective-permute-done | bytes 524320 | tf_op jit(solution)/shard_map/ppermute | solution.py:323
  228.8 1.9 fusion.12
  231.6 1.6 collective-permute-start.29
  233.2 3.0 %collective-permute-start.30 = (bf16[2,128,256]{2,1,0:T(8,128)(2,1)S(1)}, bf16[2,128,256]{2,1,0:T(8,128)(2,1)S(1)}, u32[]{:S(2)}, u32[]{:S(2)}) collective-permute-start(bf16[2,128,256]{2,1,0:T(8,128)(2,1)S(1)} %get-tuple-element.46), channel_id=1, source_target_pairs={{0,12},{1,13},{2,14},{3,15},{4,16},{5,17},{6,18},{7,19},{8,20},{9,... | collective-permute-start | bytes 393224 | tf_op jit(solution)/shard_map/ppermute | solution.py:326
  236.2 3.4 %collective-permute-start.31 = (bf16[2,128,256]{2,1,0:T(8,128)(2,1)S(1)}, bf16[2,128,256]{2,1,0:T(8,128)(2,1)S(1)}, u32[]{:S(2)}, u32[]{:S(2)}) collective-permute-start(bf16[2,128,256]{2,1,0:T(8,128)(2,1)S(1)} %get-tuple-element.47), channel_id=1, source_target_pairs={{0,16},{1,17},{2,18},{3,19},{4,20},{5,21},{6,22},{7,23},{8,24},{9,... | collective-permute-start | bytes 393224 | tf_op jit(solution)/shard_map/ppermute | solution.py:326
  239.6 2.4 collective-permute-start.32
  242.8 5.5 %collective-permute-done.29 = bf16[2,128,256]{2,1,0:T(8,128)(2,1)S(1)} collective-permute-done((bf16[2,128,256]{2,1,0:T(8,128)(2,1)S(1)}, bf16[2,128,256]{2,1,0:T(8,128)(2,1)S(1)}, u32[]{:S(2)}, u32[]{:S(2)}) %collective-permute-start.29) | collective-permute-done | bytes 131104 | tf_op jit(solution)/shard_map/ppermute | solution.py:326
  248.3 13.7 %query_grad.1 = bf16[240,4096]{1,0:T(8,128)(2,1)} custom-call(s32[12]{0:T(128)} %get-tuple-element.16.slot_ref, s32[1]{0:T(128)} %bitcast.10.here_ref, bf16[6,256,1280]{2,1,0:T(8,128)(2,1)} %get-tuple-element.21.ds_ref, bf16[32,128,512]{2,1,0:T(8,128)(2,1)} %all-to-all-done.2.arrived, bf16[4,128,512]{2,1,0:T(8,128)(2,1)} %copy-done, ...), custom_call_target="tpu_custom_call" | custom-call | flops 3000000000 | bytes 12000000 | tf_op jit(solution)/shard_map/query_grad/pallas_call | solution.py:244
  262.1 1.3 fusion
  (121 shorter events, 15.1 us)
Async XLA Ops:
  2.6 25.0 %copy-start.17 = (s32[1,6,2]{1,2,0:T(2,128)S(1)}, s32[1,6,2]{1,2,0:T(2,128)}, u32[]{:S(2)}) copy-start(s32[1,6,2]{1,2,0:T(2,128)} %param.13) | copy-start | bytes 148
  3.8 19.1 %all-to-all-start = ((bf16[4,2,128,512]{3,2,1,0:T(8,128)(2,1)}), bf16[4,2,128,512]{3,2,1,0:T(8,128)(2,1)S(1)}, u32[]{:S(2)}, u32[]{:S(2)}) async-start(bf16[4,2,128,512]{3,2,1,0:T(8,128)(2,1)} %broadcast_in_dim.72), calls=%async_computation | async-start | bytes 2097152 | tf_op jit(solution)/shard_map/all_to_all | solution.py:320
  8.5 10.9 %collective-permute-start.2 = (bf16[2,128,512]{2,1,0:T(8,128)(2,1)S(1)}, bf16[2,128,512]{2,1,0:T(8,128)(2,1)S(1)}, u32[]{:S(2)}, u32[]{:S(2)}) collective-permute-start(bf16[2,128,512]{2,1,0:T(8,128)(2,1)S(1)} %bitcast.92), channel_id=1, source_target_pairs={{0,28},{1,29},{2,30},{3,31},{4,0},{5,1},{6,2},{7,3},{8,4},{9,5},{1... | collective-permute-start | bytes 786440 | tf_op jit(solution)/shard_map/ppermute | solution.py:326
  14.4 8.4 %collective-permute-start.1 = (bf16[2,128,512]{2,1,0:T(8,128)(2,1)S(1)}, bf16[2,128,512]{2,1,0:T(8,128)(2,1)S(1)}, u32[]{:S(2)}, u32[]{:S(2)}) collective-permute-start(bf16[2,128,512]{2,1,0:T(8,128)(2,1)S(1)} %bitcast.93), channel_id=1, source_target_pairs={{0,4},{1,5},{2,6},{3,7},{4,8},{5,9},{6,10},{7,11},{8,12},{9,13},{1... | collective-permute-start | bytes 786440 | tf_op jit(solution)/shard_map/ppermute | solution.py:326
  19.4 36.4 %copy-start.11 = (bf16[2,128,512]{2,1,0:T(8,128)(2,1)}, bf16[2,128,512]{2,1,0:T(8,128)(2,1)S(1)}, u32[]{:S(2)}) copy-start(bf16[2,128,512]{2,1,0:T(8,128)(2,1)S(1)} %collective-permute-done.2.refs_7_) | copy-start | bytes 786436
  22.8 33.0 %copy-start.12 = (bf16[2,128,512]{2,1,0:T(8,128)(2,1)}, bf16[2,128,512]{2,1,0:T(8,128)(2,1)S(1)}, u32[]{:S(2)}) copy-start(bf16[2,128,512]{2,1,0:T(8,128)(2,1)S(1)} %collective-permute-done.1.refs_1_) | copy-start | bytes 786436
  22.8 9.8 %collective-permute-start.3 = (bf16[2,128,512]{2,1,0:T(8,128)(2,1)S(1)}, bf16[2,128,512]{2,1,0:T(8,128)(2,1)S(1)}, u32[]{:S(2)}, u32[]{:S(2)}) collective-permute-start(bf16[2,128,512]{2,1,0:T(8,128)(2,1)S(1)} %collective-permute-done.1.refs_1_), channel_id=1, source_target_pairs={{0,4},{1,5},{2,6},{3,7},{4,8},{5,9},{6,10},{7,11},{8,12},{9,13},{1... | collective-permute-start | bytes 786440 | tf_op jit(solution)/shard_map/ppermute | solution.py:326
  23.5 9.1 %collective-permute-start.6 = (bf16[2,128,512]{2,1,0:T(8,128)(2,1)S(1)}, bf16[2,128,512]{2,1,0:T(8,128)(2,1)S(1)}, u32[]{:S(2)}, u32[]{:S(2)}) collective-permute-start(bf16[2,128,512]{2,1,0:T(8,128)(2,1)S(1)} %collective-permute-done.2.refs_7_), channel_id=1, source_target_pairs={{0,28},{1,29},{2,30},{3,31},{4,0},{5,1},{6,2},{7,3},{8,4},{9,5},{1... | collective-permute-start | bytes 786440 | tf_op jit(solution)/shard_map/ppermute | solution.py:326
  27.6 92.0 %copy-start.15 = (s32[12]{0:T(128)}, s32[12]{0:T(128)S(1)}, u32[]{:S(2)}) copy-start(s32[12]{0:T(128)S(1)} %reshape_squeeze.3.dense_slot) | copy-start | bytes 148
  32.6 12.5 %collective-permute-start.4 = (bf16[2,128,512]{2,1,0:T(8,128)(2,1)S(1)}, bf16[2,128,512]{2,1,0:T(8,128)(2,1)S(1)}, u32[]{:S(2)}, u32[]{:S(2)}) collective-permute-start(bf16[2,128,512]{2,1,0:T(8,128)(2,1)S(1)} %collective-permute-done.3.refs_2_), channel_id=1, source_target_pairs={{0,4},{1,5},{2,6},{3,7},{4,8},{5,9},{6,10},{7,11},{8,12},{9,13},{1... | collective-permute-start | bytes 786440 | tf_op jit(solution)/shard_map/ppermute | solution.py:326
  32.6 14.0 %collective-permute-start.7 = (bf16[2,128,512]{2,1,0:T(8,128)(2,1)S(1)}, bf16[2,128,512]{2,1,0:T(8,128)(2,1)S(1)}, u32[]{:S(2)}, u32[]{:S(2)}) collective-permute-start(bf16[2,128,512]{2,1,0:T(8,128)(2,1)S(1)} %collective-permute-done.6.refs_6_), channel_id=1, source_target_pairs={{0,28},{1,29},{2,30},{3,31},{4,0},{5,1},{6,2},{7,3},{8,4},{9,5},{1... | collective-permute-start | bytes 786440 | tf_op jit(solution)/shard_map/ppermute | solution.py:326
  36.6 16.6 %all-to-all-start.1 = ((s32[32,1,8]{2,1,0:T(1,128)}), s32[32,1,8]{2,1,0:T(1,128)S(1)}, u32[]{:S(2)}, u32[]{:S(2)}) async-start(s32[32,1,8]{2,1,0:T(1,128)} %bitcast.5), calls=%async_computation.1 | async-start | bytes 32768 | tf_op jit(solution)/shard_map/all_to_all | solution.py:320
  45.1 10.0 %collective-permute-start.5 = (bf16[1,128,512]{2,1,0:T(8,128)(2,1)S(1)}, bf16[1,128,512]{2,1,0:T(8,128)(2,1)S(1)}, u32[]{:S(2)}, u32[]{:S(2)}) collective-permute-start(bf16[1,128,512]{2,1,0:T(8,128)(2,1)S(1)} %slice.84), channel_id=1, source_target_pairs={{0,4},{1,5},{2,6},{3,7},{4,8},{5,9},{6,10},{7,11},{8,12},{9,13},{1... | collective-permute-start | bytes 393224 | tf_op jit(solution)/shard_map/ppermute | solution.py:326
  46.6 8.5 %collective-permute-start.8 = (bf16[1,128,512]{2,1,0:T(8,128)(2,1)S(1)}, bf16[1,128,512]{2,1,0:T(8,128)(2,1)S(1)}, u32[]{:S(2)}, u32[]{:S(2)}) collective-permute-start(bf16[1,128,512]{2,1,0:T(8,128)(2,1)S(1)} %slice.85), channel_id=1, source_target_pairs={{0,28},{1,29},{2,30},{3,31},{4,0},{5,1},{6,2},{7,3},{8,4},{9,5},{1... | collective-permute-start | bytes 393224 | tf_op jit(solution)/shard_map/ppermute | solution.py:326
  61.3 89.3 %all-to-all-start.2 = ((bf16[32,128,512]{2,1,0:T(8,128)(2,1)}), bf16[32,128,512]{2,1,0:T(8,128)(2,1)}, u32[]{:S(2)}, u32[]{:S(2)}) async-start(bf16[32,128,512]{2,1,0:T(8,128)(2,1)} %serve.1), calls=%async_computation.2 | async-start | bytes 8388608 | tf_op jit(solution)/shard_map/all_to_all | solution.py:320
  68.2 82.5 %copy-start = (bf16[4,128,512]{2,1,0:T(8,128)(2,1)}, bf16[4,128,512]{2,1,0:T(8,128)(2,1)S(1)}, u32[]{:S(2)}) copy-start(bf16[4,128,512]{2,1,0:T(8,128)(2,1)S(1)} %get-tuple-element.52.refs_0_) | copy-start | bytes 1572868
  68.2 14.9 %collective-permute-start.18 = (bf16[4,128,512]{2,1,0:T(8,128)(2,1)S(1)}, bf16[4,128,512]{2,1,0:T(8,128)(2,1)S(1)}, u32[]{:S(2)}, u32[]{:S(2)}) collective-permute-start(bf16[4,128,512]{2,1,0:T(8,128)(2,1)S(1)} %get-tuple-element.51.refs_9_), channel_id=1, source_target_pairs={{0,28},{1,29},{2,30},{3,31},{4,0},{5,1},{6,2},{7,3},{8,4},{9,5},{1... | collective-permute-start | bytes 1572872 | tf_op jit(solution)/shard_map/ppermute | solution.py:326
  69.1 16.0 %collective-permute-start.17 = (bf16[4,128,512]{2,1,0:T(8,128)(2,1)S(1)}, bf16[4,128,512]{2,1,0:T(8,128)(2,1)S(1)}, u32[]{:S(2)}, u32[]{:S(2)}) collective-permute-start(bf16[4,128,512]{2,1,0:T(8,128)(2,1)S(1)} %get-tuple-element.51.refs_9_), channel_id=1, source_target_pairs={{0,4},{1,5},{2,6},{3,7},{4,8},{5,9},{6,10},{7,11},{8,12},{9,13},{1... | collective-permute-start | bytes 1572872 | tf_op jit(solution)/shard_map/ppermute | solution.py:326
  70.3 24.0 %collective-permute-start.10 = (bf16[4,128,512]{2,1,0:T(8,128)(2,1)S(1)}, bf16[4,128,512]{2,1,0:T(8,128)(2,1)S(1)}, u32[]{:S(2)}, u32[]{:S(2)}) collective-permute-start(bf16[4,128,512]{2,1,0:T(8,128)(2,1)S(1)} %get-tuple-element.52.refs_0_), channel_id=1, source_target_pairs={{0,28},{1,29},{2,30},{3,31},{4,0},{5,1},{6,2},{7,3},{8,4},{9,5},{1... | collective-permute-start | bytes 1572872 | tf_op jit(solution)/shard_map/ppermute | solution.py:326
  72.4 24.0 %collective-permute-start.9 = (bf16[4,128,512]{2,1,0:T(8,128)(2,1)S(1)}, bf16[4,128,512]{2,1,0:T(8,128)(2,1)S(1)}, u32[]{:S(2)}, u32[]{:S(2)}) collective-permute-start(bf16[4,128,512]{2,1,0:T(8,128)(2,1)S(1)} %get-tuple-element.52.refs_0_), channel_id=1, source_target_pairs={{0,4},{1,5},{2,6},{3,7},{4,8},{5,9},{6,10},{7,11},{8,12},{9,13},{1... | collective-permute-start | bytes 1572872 | tf_op jit(solution)/shard_map/ppermute | solution.py:326
  72.4 72.0 %collective-permute-start = (bf16[1,240,4096]{2,1,0:T(8,128)(2,1)}, bf16[1,240,4096]{2,1,0:T(8,128)(2,1)}, u32[]{:S(2)}, u32[]{:S(2)}) collective-permute-start(bf16[1,240,4096]{2,1,0:T(8,128)(2,1)} %param.8), channel_id=1, source_target_pairs={{0,224},{32,0},{64,32},{96,64},{128,96},{160,128},{192,160},{224,1... | collective-permute-start | bytes 5898248 | tf_op jit(solution)/shard_map/ppermute | solution.py:363
  83.1 22.6 %collective-permute-start.20 = (bf16[4,128,512]{2,1,0:T(8,128)(2,1)S(1)}, bf16[4,128,512]{2,1,0:T(8,128)(2,1)}, u32[]{:S(2)}, u32[]{:S(2)}) collective-permute-start(bf16[4,128,512]{2,1,0:T(8,128)(2,1)S(1)} %collective-permute-done.18.refs_11_), channel_id=1, source_target_pairs={{0,28},{1,29},{2,30},{3,31},{4,0},{5,1},{6,2},{7,3},{8,4},{9,5},{1... | collective-permute-start | bytes 1572872 | tf_op jit(solution)/shard_map/ppermute | solution.py:326
  85.1 33.7 %copy-start.19 = (bf16[4,128,512]{2,1,0:T(8,128)(2,1)}, bf16[4,128,512]{2,1,0:T(8,128)(2,1)S(1)}, u32[]{:S(2)}) copy-start(bf16[4,128,512]{2,1,0:T(8,128)(2,1)S(1)} %collective-permute-done.17.refs_10_) | copy-start | bytes 1572868
  85.1 22.6 %collective-permute-start.19 = (bf16[4,128,512]{2,1,0:T(8,128)(2,1)S(1)}, bf16[4,128,512]{2,1,0:T(8,128)(2,1)}, u32[]{:S(2)}, u32[]{:S(2)}) collective-permute-start(bf16[4,128,512]{2,1,0:T(8,128)(2,1)S(1)} %collective-permute-done.17.refs_10_), channel_id=1, source_target_pairs={{0,4},{1,5},{2,6},{3,7},{4,8},{5,9},{6,10},{7,11},{8,12},{9,13},{1... | collective-permute-start | bytes 1572872 | tf_op jit(solution)/shard_map/ppermute | solution.py:326
  94.3 56.4 %copy-start.5 = (bf16[4,128,512]{2,1,0:T(8,128)(2,1)}, bf16[4,128,512]{2,1,0:T(8,128)(2,1)S(1)}, u32[]{:S(2)}) copy-start(bf16[4,128,512]{2,1,0:T(8,128)(2,1)S(1)} %collective-permute-done.10.refs_2_) | copy-start | bytes 1572868
  94.3 22.5 %collective-permute-start.12 = (bf16[4,128,512]{2,1,0:T(8,128)(2,1)S(1)}, bf16[4,128,512]{2,1,0:T(8,128)(2,1)S(1)}, u32[]{:S(2)}, u32[]{:S(2)}) collective-permute-start(bf16[4,128,512]{2,1,0:T(8,128)(2,1)S(1)} %collective-permute-done.10.refs_2_), channel_id=1, source_target_pairs={{0,28},{1,29},{2,30},{3,31},{4,0},{5,1},{6,2},{7,3},{8,4},{9,5},{1... | collective-permute-start | bytes 1572872 | tf_op jit(solution)/shard_map/ppermute | solution.py:326
  96.4 54.3 %copy-start.6 = (bf16[4,128,512]{2,1,0:T(8,128)(2,1)}, bf16[4,128,512]{2,1,0:T(8,128)(2,1)S(1)}, u32[]{:S(2)}) copy-start(bf16[4,128,512]{2,1,0:T(8,128)(2,1)S(1)} %collective-permute-done.9.refs_1_) | copy-start | bytes 1572868
  96.4 22.6 %collective-permute-start.11 = (bf16[4,128,512]{2,1,0:T(8,128)(2,1)S(1)}, bf16[4,128,512]{2,1,0:T(8,128)(2,1)}, u32[]{:S(2)}, u32[]{:S(2)}) collective-permute-start(bf16[4,128,512]{2,1,0:T(8,128)(2,1)S(1)} %collective-permute-done.9.refs_1_), channel_id=1, source_target_pairs={{0,4},{1,5},{2,6},{3,7},{4,8},{5,9},{6,10},{7,11},{8,12},{9,13},{1... | collective-permute-start | bytes 1572872 | tf_op jit(solution)/shard_map/ppermute | solution.py:326
  105.6 22.5 %collective-permute-start.22 = (bf16[4,128,512]{2,1,0:T(8,128)(2,1)}, bf16[4,128,512]{2,1,0:T(8,128)(2,1)}, u32[]{:S(2)}, u32[]{:S(2)}) collective-permute-start(bf16[4,128,512]{2,1,0:T(8,128)(2,1)} %collective-permute-done.20.refs_13_), channel_id=1, source_target_pairs={{0,28},{1,29},{2,30},{3,31},{4,0},{5,1},{6,2},{7,3},{8,4},{9,5},{1... | collective-permute-start | bytes 1572872 | tf_op jit(solution)/shard_map/ppermute | solution.py:326
  107.7 24.2 %collective-permute-start.21 = (bf16[4,128,512]{2,1,0:T(8,128)(2,1)}, bf16[4,128,512]{2,1,0:T(8,128)(2,1)}, u32[]{:S(2)}, u32[]{:S(2)}) collective-permute-start(bf16[4,128,512]{2,1,0:T(8,128)(2,1)} %collective-permute-done.19.refs_12_), channel_id=1, source_target_pairs={{0,4},{1,5},{2,6},{3,7},{4,8},{5,9},{6,10},{7,11},{8,12},{9,13},{1... | collective-permute-start | bytes 1572872 | tf_op jit(solution)/shard_map/ppermute | solution.py:326
  116.8 33.9 %copy-start.7 = (bf16[4,128,512]{2,1,0:T(8,128)(2,1)}, bf16[4,128,512]{2,1,0:T(8,128)(2,1)S(1)}, u32[]{:S(2)}) copy-start(bf16[4,128,512]{2,1,0:T(8,128)(2,1)S(1)} %collective-permute-done.12.refs_4_) | copy-start | bytes 1572868
  116.8 22.5 %collective-permute-start.14 = (bf16[4,128,512]{2,1,0:T(8,128)(2,1)S(1)}, bf16[4,128,512]{2,1,0:T(8,128)(2,1)S(1)}, u32[]{:S(2)}, u32[]{:S(2)}) collective-permute-start(bf16[4,128,512]{2,1,0:T(8,128)(2,1)S(1)} %collective-permute-done.12.refs_4_), channel_id=1, source_target_pairs={{0,28},{1,29},{2,30},{3,31},{4,0},{5,1},{6,2},{7,3},{8,4},{9,5},{1... | collective-permute-start | bytes 1572872 | tf_op jit(solution)/shard_map/ppermute | solution.py:326
  118.9 23.0 %collective-permute-start.13 = (bf16[4,128,512]{2,1,0:T(8,128)(2,1)}, bf16[4,128,512]{2,1,0:T(8,128)(2,1)S(1)}, u32[]{:S(2)}, u32[]{:S(2)}) collective-permute-start(bf16[4,128,512]{2,1,0:T(8,128)(2,1)} %collective-permute-done.11.refs_3_), channel_id=1, source_target_pairs={{0,4},{1,5},{2,6},{3,7},{4,8},{5,9},{6,10},{7,11},{8,12},{9,13},{1... | collective-permute-start | bytes 1572872 | tf_op jit(solution)/shard_map/ppermute | solution.py:326
  129.8 14.6 %collective-permute-start.24 = (bf16[2,128,512]{2,1,0:T(8,128)(2,1)}, bf16[2,128,512]{2,1,0:T(8,128)(2,1)}, u32[]{:S(2)}, u32[]{:S(2)}) collective-permute-start(bf16[2,128,512]{2,1,0:T(8,128)(2,1)} %slice.91), channel_id=1, source_target_pairs={{0,28},{1,29},{2,30},{3,31},{4,0},{5,1},{6,2},{7,3},{8,4},{9,5},{1... | collective-permute-start | bytes 786440 | tf_op jit(solution)/shard_map/ppermute | solution.py:326
  133.6 10.8 %collective-permute-start.23 = (bf16[2,128,512]{2,1,0:T(8,128)(2,1)}, bf16[2,128,512]{2,1,0:T(8,128)(2,1)}, u32[]{:S(2)}, u32[]{:S(2)}) collective-permute-start(bf16[2,128,512]{2,1,0:T(8,128)(2,1)} %slice.90), channel_id=1, source_target_pairs={{0,4},{1,5},{2,6},{3,7},{4,8},{5,9},{6,10},{7,11},{8,12},{9,13},{1... | collective-permute-start | bytes 786440 | tf_op jit(solution)/shard_map/ppermute | solution.py:326
  140.0 6.6 %collective-permute-start.16 = (bf16[2,128,512]{2,1,0:T(8,128)(2,1)}, bf16[2,128,512]{2,1,0:T(8,128)(2,1)S(1)}, u32[]{:S(2)}, u32[]{:S(2)}) collective-permute-start(bf16[2,128,512]{2,1,0:T(8,128)(2,1)} %slice.88), channel_id=1, source_target_pairs={{0,28},{1,29},{2,30},{3,31},{4,0},{5,1},{6,2},{7,3},{8,4},{9,5},{1... | collective-permute-start | bytes 786440 | tf_op jit(solution)/shard_map/ppermute | solution.py:326
  142.8 7.9 %collective-permute-start.15 = (bf16[2,128,512]{2,1,0:T(8,128)(2,1)}, bf16[2,128,512]{2,1,0:T(8,128)(2,1)}, u32[]{:S(2)}, u32[]{:S(2)}) collective-permute-start(bf16[2,128,512]{2,1,0:T(8,128)(2,1)} %slice.87), channel_id=1, source_target_pairs={{0,4},{1,5},{2,6},{3,7},{4,8},{5,9},{6,10},{7,11},{8,12},{9,13},{1... | collective-permute-start | bytes 786440 | tf_op jit(solution)/shard_map/ppermute | solution.py:326
  181.3 80.8 %all-to-all-start.3 = ((bf16[32,128,256]{2,1,0:T(8,128)(2,1)}), bf16[32,128,256]{2,1,0:T(8,128)(2,1)S(1)}, u32[]{:S(2)}, u32[]{:S(2)}) async-start(bf16[32,128,256]{2,1,0:T(8,128)(2,1)} %get-tuple-element.25), calls=%async_computation.3 | async-start | bytes 4194304 | tf_op jit(solution)/shard_map/all_to_all | solution.py:320
  190.0 25.8 %collective-permute-start.25 = (bf16[8,128,256]{2,1,0:T(8,128)(2,1)S(1)}, bf16[8,128,256]{2,1,0:T(8,128)(2,1)S(1)}, u32[]{:S(2)}, u32[]{:S(2)}) collective-permute-start(bf16[8,128,256]{2,1,0:T(8,128)(2,1)S(1)} %get-tuple-element.41), channel_id=1, source_target_pairs={{0,1},{1,2},{2,3},{3,0},{4,5},{5,6},{6,7},{7,4},{8,9},{9,10},{10,1... | collective-permute-start | bytes 1572872 | tf_op jit(solution)/shard_map/ppermute | solution.py:323
  190.3 25.5 %collective-permute-start.27 = (bf16[8,128,256]{2,1,0:T(8,128)(2,1)S(1)}, bf16[8,128,256]{2,1,0:T(8,128)(2,1)S(1)}, u32[]{:S(2)}, u32[]{:S(2)}) collective-permute-start(bf16[8,128,256]{2,1,0:T(8,128)(2,1)S(1)} %get-tuple-element.42), channel_id=1, source_target_pairs={{0,3},{1,0},{2,1},{3,2},{4,7},{5,4},{6,5},{7,6},{8,11},{9,8},{10,9... | collective-permute-start | bytes 1572872 | tf_op jit(solution)/shard_map/ppermute | solution.py:323
  192.1 36.7 %collective-permute-start.26 = (bf16[8,128,256]{2,1,0:T(8,128)(2,1)S(1)}, bf16[8,128,256]{2,1,0:T(8,128)(2,1)S(1)}, u32[]{:S(2)}, u32[]{:S(2)}) collective-permute-start(bf16[8,128,256]{2,1,0:T(8,128)(2,1)S(1)} %get-tuple-element.43), channel_id=1, source_target_pairs={{0,2},{1,3},{2,0},{3,1},{4,6},{5,7},{6,4},{7,5},{8,10},{9,11},{10,... | collective-permute-start | bytes 1572872 | tf_op jit(solution)/shard_map/ppermute | solution.py:323
  230.8 11.3 %collective-permute-start.28 = (bf16[2,128,256]{2,1,0:T(8,128)(2,1)S(1)}, bf16[2,128,256]{2,1,0:T(8,128)(2,1)S(1)}, u32[]{:S(2)}, u32[]{:S(2)}) collective-permute-start(bf16[2,128,256]{2,1,0:T(8,128)(2,1)S(1)} %get-tuple-element.44), channel_id=1, source_target_pairs={{0,4},{1,5},{2,6},{3,7},{4,8},{5,9},{6,10},{7,11},{8,12},{9,13},{1... | collective-permute-start | bytes 393224 | tf_op jit(solution)/shard_map/ppermute | solution.py:326
  231.6 16.6 %collective-permute-start.29 = (bf16[2,128,256]{2,1,0:T(8,128)(2,1)S(1)}, bf16[2,128,256]{2,1,0:T(8,128)(2,1)S(1)}, u32[]{:S(2)}, u32[]{:S(2)}) collective-permute-start(bf16[2,128,256]{2,1,0:T(8,128)(2,1)S(1)} %get-tuple-element.45), channel_id=1, source_target_pairs={{0,8},{1,9},{2,10},{3,11},{4,12},{5,13},{6,14},{7,15},{8,16},{9,17... | collective-permute-start | bytes 393224 | tf_op jit(solution)/shard_map/ppermute | solution.py:326
  233.2 28.7 %collective-permute-start.30 = (bf16[2,128,256]{2,1,0:T(8,128)(2,1)S(1)}, bf16[2,128,256]{2,1,0:T(8,128)(2,1)S(1)}, u32[]{:S(2)}, u32[]{:S(2)}) collective-permute-start(bf16[2,128,256]{2,1,0:T(8,128)(2,1)S(1)} %get-tuple-element.46), channel_id=1, source_target_pairs={{0,12},{1,13},{2,14},{3,15},{4,16},{5,17},{6,18},{7,19},{8,20},{9,... | collective-permute-start | bytes 393224 | tf_op jit(solution)/shard_map/ppermute | solution.py:326
  236.2 25.8 %collective-permute-start.31 = (bf16[2,128,256]{2,1,0:T(8,128)(2,1)S(1)}, bf16[2,128,256]{2,1,0:T(8,128)(2,1)S(1)}, u32[]{:S(2)}, u32[]{:S(2)}) collective-permute-start(bf16[2,128,256]{2,1,0:T(8,128)(2,1)S(1)} %get-tuple-element.47), channel_id=1, source_target_pairs={{0,16},{1,17},{2,18},{3,19},{4,20},{5,21},{6,22},{7,23},{8,24},{9,... | collective-permute-start | bytes 393224 | tf_op jit(solution)/shard_map/ppermute | solution.py:326
  239.6 22.3 %collective-permute-start.32 = (bf16[2,128,256]{2,1,0:T(8,128)(2,1)S(1)}, bf16[2,128,256]{2,1,0:T(8,128)(2,1)S(1)}, u32[]{:S(2)}, u32[]{:S(2)}) collective-permute-start(bf16[2,128,256]{2,1,0:T(8,128)(2,1)S(1)} %get-tuple-element.48), channel_id=1, source_target_pairs={{0,20},{1,21},{2,22},{3,23},{4,24},{5,25},{6,26},{7,27},{8,28},{9,... | collective-permute-start | bytes 393224 | tf_op jit(solution)/shard_map/ppermute | solution.py:326
  242.1 19.9 %collective-permute-start.34 = (bf16[2,128,256]{2,1,0:T(8,128)(2,1)S(1)}, bf16[2,128,256]{2,1,0:T(8,128)(2,1)S(1)}, u32[]{:S(2)}, u32[]{:S(2)}) collective-permute-start(bf16[2,128,256]{2,1,0:T(8,128)(2,1)S(1)} %get-tuple-element.49), channel_id=1, source_target_pairs={{0,28},{1,29},{2,30},{3,31},{4,0},{5,1},{6,2},{7,3},{8,4},{9,5},{1... | collective-permute-start | bytes 393224 | tf_op jit(solution)/shard_map/ppermute | solution.py:326
  248.2 13.7 %collective-permute-start.33 = (bf16[2,128,256]{2,1,0:T(8,128)(2,1)S(1)}, bf16[2,128,256]{2,1,0:T(8,128)(2,1)S(1)}, u32[]{:S(2)}, u32[]{:S(2)}) collective-permute-start(bf16[2,128,256]{2,1,0:T(8,128)(2,1)S(1)} %get-tuple-element.50), channel_id=1, source_target_pairs={{0,24},{1,25},{2,26},{3,27},{4,28},{5,29},{6,30},{7,31},{8,0},{9,1... | collective-permute-start | bytes 393224 | tf_op jit(solution)/shard_map/ppermute | solution.py:326
  (11 other events, 163.2 us)
where the time goes:
time: 265 us; the launch traced here: 264 us
  waiting for transfers between devices  116 us (44%)
  starting transfers between devices  76.3 us (29%)
  Pallas kernels  49.7 us (19%)
  local copies, waits for them, and re-layouts  13.9 us (5%)
  other arithmetic  6.2 us (2%)
    ppermute x31, waiting for transfers between devices, send_z(): return lax.ppermute(v, 'dp', pairs_z(groups, shift))  76.1 us
    ppermute x31, starting transfers between devices, send_z(): return lax.ppermute(v, 'dp', pairs_z(groups, shift))  45.6 us
    ppermute x3, waiting for transfers between devices, send_x(): return lax.ppermute(v, 'dp', pairs_x(groups, shift))  35 us
    pallas_call x1, Pallas kernels, grads_call(): pl.pallas_call(functools.partial(grads_kernel, heads, pieces), grid_spec=...  30.6 us
    all_to_all x4, starting transfers between devices, exchange(): lax.all_to_all(v, 'dp', split_axis=0, concat_axis=0, tiled=True, axis_ind...  27.1 us
    pallas_call x1, Pallas kernels, query_call(): pl.pallas_call(functools.partial(query_kernel, heads, pieces), grid_spec=...  13.7 us
    pallas_call x1, Pallas kernels, serve_call(): pl.pallas_call(serve_kernel, in_specs=[pl.BlockSpec(memory_space=pltpu.SM...  5.47 us
  transfers between devices with their start and end apart: 39, of which 16 were waited for; matrix products, arithmetic and copies ran while one was open for 6% of the time, Pallas kernels for 5%

commit v1 on v0

--- a/solution.py
+++ b/solution.py
@@ -53,8 +53,9 @@
 
 def grads_kernel(heads, pieces, slot_ref, here_ref, row_slot, dense_slot, first_ref, q_ref, g_ref, arrived, *refs):
     key_ring, value_ring = refs[:pieces], refs[pieces : 2 * pieces]
-    ds_ref, row_ref, dense_ref = refs[2 * pieces : 2 * pieces + 3]
-    key_w, value_w, keys_ref, a_ref, b_ref, sum_ref, sem_k, sem_v, sem_e = refs[2 * pieces + 3 :]
+    ds_ref, dense_ref = refs[2 * pieces : 2 * pieces + 2]
+    row_refs = refs[2 * pieces + 2 : 2 * pieces + 2 + NX]
+    key_w, value_w, keys_ref, a_ref, b_ref, sum_ref, sem_k, sem_v, sem_e = refs[2 * pieces + 2 + NX :]
     step = pl.program_id(0)
     here = here_ref[0]
     of_keys = weight_copies(here, key_ring, key_w, sem_k)
@@ -66,10 +67,13 @@
         for copy in of_keys + of_values + of_rows:
             copy.start()
 
-        @pl.loop(0, row_ref.shape[0])
+        blank = jnp.zeros(dense_ref.shape[1:], BF16)
+
+        @pl.loop(0, row_refs[0].shape[0])
         def _(n):
-            row_ref[n] = jnp.zeros(row_ref.shape[1:], BF16)
-            dense_ref[n] = jnp.zeros(row_ref.shape[1:], BF16)
+            for x, row_ref in enumerate(row_refs):
+                row_ref[n] = blank
+                dense_ref[n * NX + x] = blank
 
     spans = a_ref.shape[0]
     quad = key_w.shape[2] // HEAD_DIM
@@ -125,8 +129,9 @@
 
     @pl.when(step == pl.num_programs(0) - 1)
     def _():
-        length = row_ref.shape[1]
-        half = row_ref.shape[2]
+        length = dense_ref.shape[1]
+        half = dense_ref.shape[2]
+        nz = row_refs[0].shape[0]
         per = sum_ref.shape[1] // length
 
         def rows_of(n):
@@ -146,7 +151,13 @@
             @pl.when(first_ref[n] == n)
             def _():
                 value = sum_ref[rows_of(n)].astype(BF16)
-                row_ref[row_slot[n]] = value[:, :half]
+                for x, row_ref in enumerate(row_refs):
+                    at = row_slot[n] - x * nz
+
+                    @pl.when((at >= 0) & (at < nz))
+                    def _():
+                        row_ref[at] = value[:, :half]
+
                 dense_ref[dense_slot[n]] = value[:, half:]
 
 
@@ -162,6 +173,7 @@
     wide = (ranks,) + key_ring[0].shape[1:]
     anywhere = pl.BlockSpec(memory_space=pl.ANY)
     whole = pl.BlockSpec((ranks, rows, enc // 2), lambda i, *_: (0, 0, 0))
+    piece = pl.BlockSpec((ranks // NX, rows, enc // 2), lambda i, *_: (0, 0, 0))
     return pl.pallas_call(
         functools.partial(grads_kernel, heads, pieces),
         grid_spec=pltpu.PrefetchScalarGridSpec(
@@ -172,7 +184,7 @@
                 pl.BlockSpec((tok, cols), lambda i, *_: (0, i)),
             ]
             + [anywhere] * (1 + 2 * pieces),
-            out_specs=[pl.BlockSpec((spans, kr, m), lambda i, *_: (0, 0, i)), whole, whole],
+            out_specs=[pl.BlockSpec((spans, kr, m), lambda i, *_: (0, 0, i)), whole] + [piece] * NX,
             scratch_shapes=[
                 pltpu.VMEM(wide, BF16),
                 pltpu.VMEM(wide, BF16),
@@ -188,11 +200,11 @@
         out_shape=[
             jax.ShapeDtypeStruct((spans, kr, m * groups), BF16),
             jax.ShapeDtypeStruct((ranks, rows, enc // 2), BF16),
-            jax.ShapeDtypeStruct((ranks, rows, enc // 2), BF16),
-        ],
+        ]
+        + [jax.ShapeDtypeStruct((ranks // NX, rows, enc // 2), BF16)] * NX,
         name="grads",
         cost_estimate=pl.CostEstimate(flops=10**10, bytes_accessed=25 * 10**6, transcendentals=2 * 10**6),
-        compiler_params=pltpu.CompilerParams(vmem_limit_bytes=56 << 20),
+        compiler_params=pltpu.CompilerParams(vmem_limit_bytes=60 << 20),
     )(slots, here, row_slot, dense_slot, first, q, g, arrived, *key_ring, *value_ring)
 
 
@@ -373,13 +385,13 @@
         (slots, first, row_slot, wanted, row_blocks)
     )
 
-    ds, part, dense = grads_call(
-        slots, at, row_slot, owners, first, queries[0], incoming, arrived, keys, values, spans, 2
+    ds, dense, *parts = grads_call(
+        slots, at, row_slot, owners, first, queries[0], incoming, arrived, keys, values, spans, 1
     )
     returned = exchange(dense)
-    pieces = [part[:nz]]
+    pieces = [parts[0]]
     for shift in range(1, NX):
-        pieces.append(send_x(part[shift * nz : (shift + 1) * nz], shift))
+        pieces.append(send_x(parts[shift], shift))
     query_grad = query_call(slots, at, ds, arrived, keys, 2)
 
     held_ids = jnp.arange(held, dtype=jnp.int32)

time: 265 us -> 264 us (level)
  the two profiles are of different devices: /device:TPU:22 before, /device:TPU:3 now
where the time goes in v1:
time: 264 us; the launch traced here: 261 us
  waiting for transfers between devices  114 us (43%)
  starting transfers between devices  80.1 us (30%)
  Pallas kernels  47.1 us (18%)
  local copies, waits for them, and re-layouts  12.3 us (5%)
  other arithmetic  5.23 us (2%)
    ppermute x31, waiting for transfers between devices, send_z(): return lax.ppermute(v, 'dp', pairs_z(groups, shift))  68.2 us
    ppermute x31, starting transfers between devices, send_z(): return lax.ppermute(v, 'dp', pairs_z(groups, shift))  46.2 us
    ppermute x3, waiting for transfers between devices, send_x(): return lax.ppermute(v, 'dp', pairs_x(groups, shift))  41.3 us
    pallas_call x1, Pallas kernels, grads_call(): pl.pallas_call(functools.partial(grads_kernel, heads, pieces), grid_spec=...  28 us
    all_to_all x4, starting transfers between devices, exchange(): lax.all_to_all(v, 'dp', split_axis=0, concat_axis=0, tiled=True, axis_ind...  24.1 us
    pallas_call x1, Pallas kernels, query_call(): pl.pallas_call(functools.partial(query_kernel, heads, pieces), grid_spec=...  13.7 us
    ppermute x1, starting transfers between devices, shards(): lax.ppermute(out_grad, 'pipe', [(s, (s - 1) % pipe) for s in range(pipe)])  5.85 us
    pallas_call x1, Pallas kernels, serve_call(): pl.pallas_call(serve_kernel, in_specs=[pl.BlockSpec(memory_space=pltpu.SM...  5.41 us
  transfers between devices with their start and end apart: 39, of which 17 were waited for; matrix products, arithmetic and copies ran while one was open for 5% of the time, Pallas kernels for 5%

profile of v1, /device:TPU:3, one launch (start us, length us, event | category | flops | bytes accessed | tf_op | source)
XLA Modules:
  0.0 261.3 jit_solution(9674458099221930598)
XLA Ops:
  2.7 1.1 broadcast_in_dim.72
  3.8 4.3 %all-to-all-start = ((bf16[4,2,128,512]{3,2,1,0:T(8,128)(2,1)}), bf16[4,2,128,512]{3,2,1,0:T(8,128)(2,1)S(1)}, u32[]{:S(2)}, u32[]{:S(2)}) async-start(bf16[4,2,128,512]{3,2,1,0:T(8,128)(2,1)} %broadcast_in_dim.72), calls=%async_computation | async-start | bytes 2097152 | tf_op jit(solution)/shard_map/all_to_all | solution.py:332
  8.0 5.6 %collective-permute-start.2 = (bf16[2,128,512]{2,1,0:T(8,128)(2,1)S(1)}, bf16[2,128,512]{2,1,0:T(8,128)(2,1)S(1)}, u32[]{:S(2)}, u32[]{:S(2)}) collective-permute-start(bf16[2,128,512]{2,1,0:T(8,128)(2,1)S(1)} %bitcast.92), channel_id=1, source_target_pairs={{0,28},{1,29},{2,30},{3,31},{4,0},{5,1},{6,2},{7,3},{8,4},{9,5},{1... | collective-permute-start | bytes 786440 | tf_op jit(solution)/shard_map/ppermute | solution.py:338
  13.6 4.4 %collective-permute-done.2.refs_7_ = bf16[2,128,512]{2,1,0:T(8,128)(2,1)S(1)} collective-permute-done((bf16[2,128,512]{2,1,0:T(8,128)(2,1)S(1)}, bf16[2,128,512]{2,1,0:T(8,128)(2,1)S(1)}, u32[]{:S(2)}, u32[]{:S(2)}) %collective-permute-start.2) | collective-permute-done | bytes 262176 | tf_op jit(solution)/shard_map/ppermute | solution.py:338
  18.0 3.1 %collective-permute-done.1.refs_1_ = bf16[2,128,512]{2,1,0:T(8,128)(2,1)S(1)} collective-permute-done((bf16[2,128,512]{2,1,0:T(8,128)(2,1)S(1)}, bf16[2,128,512]{2,1,0:T(8,128)(2,1)S(1)}, u32[]{:S(2)}, u32[]{:S(2)}) %collective-permute-start.1) | collective-permute-done | bytes 262176 | tf_op jit(solution)/shard_map/ppermute | solution.py:338
  21.2 1.6 collective-permute-start.3
  22.7 3.9 %collective-permute-start.6 = (bf16[2,128,512]{2,1,0:T(8,128)(2,1)S(1)}, bf16[2,128,512]{2,1,0:T(8,128)(2,1)S(1)}, u32[]{:S(2)}, u32[]{:S(2)}) collective-permute-start(bf16[2,128,512]{2,1,0:T(8,128)(2,1)S(1)} %collective-permute-done.2.refs_7_), channel_id=1, source_target_pairs={{0,28},{1,29},{2,30},{3,31},{4,0},{5,1},{6,2},{7,3},{8,4},{9,5},{1... | collective-permute-start | bytes 786440 | tf_op jit(solution)/shard_map/ppermute | solution.py:338
  27.0 4.5 %collective-permute-done.3.refs_2_ = bf16[2,128,512]{2,1,0:T(8,128)(2,1)S(1)} collective-permute-done((bf16[2,128,512]{2,1,0:T(8,128)(2,1)S(1)}, bf16[2,128,512]{2,1,0:T(8,128)(2,1)S(1)}, u32[]{:S(2)}, u32[]{:S(2)}) %collective-permute-start.3) | collective-permute-done | bytes 262176 | tf_op jit(solution)/shard_map/ppermute | solution.py:338
  31.6 2.7 %collective-permute-start.7 = (bf16[2,128,512]{2,1,0:T(8,128)(2,1)S(1)}, bf16[2,128,512]{2,1,0:T(8,128)(2,1)S(1)}, u32[]{:S(2)}, u32[]{:S(2)}) collective-permute-start(bf16[2,128,512]{2,1,0:T(8,128)(2,1)S(1)} %collective-permute-done.6.refs_6_), channel_id=1, source_target_pairs={{0,28},{1,29},{2,30},{3,31},{4,0},{5,1},{6,2},{7,3},{8,4},{9,5},{1... | collective-permute-start | bytes 786440 | tf_op jit(solution)/shard_map/ppermute | solution.py:338
  35.0 6.9 %all-to-all-start.1 = ((s32[32,1,8]{2,1,0:T(1,128)}), s32[32,1,8]{2,1,0:T(1,128)S(1)}, u32[]{:S(2)}, u32[]{:S(2)}) async-start(s32[32,1,8]{2,1,0:T(1,128)} %bitcast.5), calls=%async_computation.1 | async-start | bytes 32768 | tf_op jit(solution)/shard_map/all_to_all | solution.py:332
  42.0 1.3 collective-permute-start.5
  43.3 1.6 collective-permute-start.8
  44.9 4.9 %all-to-all-done.1 = s32[32,1,8]{2,1,0:T(1,128)S(1)} async-done(((s32[32,1,8]{2,1,0:T(1,128)}), s32[32,1,8]{2,1,0:T(1,128)S(1)}, u32[]{:S(2)}, u32[]{:S(2)}) %all-to-all-start.1) | async-done | bytes 1056 | tf_op jit(solution)/shard_map/all_to_all | solution.py:332
  52.4 5.4 %serve.1 = bf16[32,128,512]{2,1,0:T(8,128)(2,1)} custom-call(s32[33]{0:T(128)} %pad_add_fusion.table_ref, bf16[2,128,512]{2,1,0:T(8,128)(2,1)} %bitcast.91, bf16[2,128,512]{2,1,0:T(8,128)(2,1)} %copy-done.13, bf16[2,128,512]{2,1,0:T(8,128)(2,1)} %copy-done.14, bf16[2,128,512]{2,1,0:T(8,128)(2,1)} %copy-done.3, ...), custom_call_target="tpu_custom_call" | custom-call | bytes 8000000 | tf_op jit(solution)/shard_map/serve/pallas_call | solution.py:296
  57.8 6.0 %all-to-all-start.2 = ((bf16[32,128,512]{2,1,0:T(8,128)(2,1)}), bf16[32,128,512]{2,1,0:T(8,128)(2,1)}, u32[]{:S(2)}, u32[]{:S(2)}) async-start(bf16[32,128,512]{2,1,0:T(8,128)(2,1)} %serve.1), calls=%async_computation.2 | async-start | bytes 8388608 | tf_op jit(solution)/shard_map/all_to_all | solution.py:332
  64.2 1.2 collective-permute-start.17
  65.4 1.5 collective-permute-start.10
  66.9 5.8 %collective-permute-start = (bf16[1,240,4096]{2,1,0:T(8,128)(2,1)}, bf16[1,240,4096]{2,1,0:T(8,128)(2,1)}, u32[]{:S(2)}, u32[]{:S(2)}) collective-permute-start(bf16[1,240,4096]{2,1,0:T(8,128)(2,1)} %param.8), channel_id=1, source_target_pairs={{0,224},{32,0},{64,32},{96,64},{128,96},{160,128},{192,160},{224,1... | collective-permute-start | bytes 5898248 | tf_op jit(solution)/shard_map/ppermute | solution.py:375
  72.7 2.9 %collective-permute-start.20 = (bf16[4,128,512]{2,1,0:T(8,128)(2,1)S(1)}, bf16[4,128,512]{2,1,0:T(8,128)(2,1)}, u32[]{:S(2)}, u32[]{:S(2)}) collective-permute-start(bf16[4,128,512]{2,1,0:T(8,128)(2,1)S(1)} %collective-permute-done.18.refs_11_), channel_id=1, source_target_pairs={{0,28},{1,29},{2,30},{3,31},{4,0},{5,1},{6,2},{7,3},{8,4},{9,5},{1... | collective-permute-start | bytes 1572872 | tf_op jit(solution)/shard_map/ppermute | solution.py:338
  75.7 8.3 %collective-permute-done.10.refs_2_ = bf16[4,128,512]{2,1,0:T(8,128)(2,1)S(1)} collective-permute-done((bf16[4,128,512]{2,1,0:T(8,128)(2,1)S(1)}, bf16[4,128,512]{2,1,0:T(8,128)(2,1)S(1)}, u32[]{:S(2)}, u32[]{:S(2)}) %collective-permute-start.10) | collective-permute-done | bytes 524320 | tf_op jit(solution)/shard_map/ppermute | solution.py:338
  84.0 1.1 collective-permute-start.12
  85.5 9.7 %collective-permute-done.20.refs_13_ = bf16[4,128,512]{2,1,0:T(8,128)(2,1)} collective-permute-done((bf16[4,128,512]{2,1,0:T(8,128)(2,1)S(1)}, bf16[4,128,512]{2,1,0:T(8,128)(2,1)}, u32[]{:S(2)}, u32[]{:S(2)}) %collective-permute-start.20) | collective-permute-done | bytes 524320 | tf_op jit(solution)/shard_map/ppermute | solution.py:338
  95.2 1.3 collective-permute-start.22
  96.7 9.8 %collective-permute-done.12.refs_4_ = bf16[4,128,512]{2,1,0:T(8,128)(2,1)S(1)} collective-permute-done((bf16[4,128,512]{2,1,0:T(8,128)(2,1)S(1)}, bf16[4,128,512]{2,1,0:T(8,128)(2,1)S(1)}, u32[]{:S(2)}, u32[]{:S(2)}) %collective-permute-start.12) | collective-permute-done | bytes 524320 | tf_op jit(solution)/shard_map/ppermute | solution.py:338
  106.5 1.1 collective-permute-start.14
  109.9 7.8 %collective-permute-done.22.refs_15_ = bf16[4,128,512]{2,1,0:T(8,128)(2,1)} collective-permute-done((bf16[4,128,512]{2,1,0:T(8,128)(2,1)}, bf16[4,128,512]{2,1,0:T(8,128)(2,1)}, u32[]{:S(2)}, u32[]{:S(2)}) %collective-permute-start.22) | collective-permute-done | bytes 524320 | tf_op jit(solution)/shard_map/ppermute | solution.py:338
  117.7 1.7 slice.75
  119.4 1.3 collective-permute-start.24
  120.6 1.7 slice.74
  122.5 6.4 %collective-permute-done.14.refs_6_ = bf16[4,128,512]{2,1,0:T(8,128)(2,1)S(1)} collective-permute-done((bf16[4,128,512]{2,1,0:T(8,128)(2,1)S(1)}, bf16[4,128,512]{2,1,0:T(8,128)(2,1)S(1)}, u32[]{:S(2)}, u32[]{:S(2)}) %collective-permute-start.14) | collective-permute-done | bytes 524320 | tf_op jit(solution)/shard_map/ppermute | solution.py:338
  129.7 1.1 collective-permute-start.16
  135.4 4.7 %collective-permute-done.16.refs_8_ = bf16[2,128,512]{2,1,0:T(8,128)(2,1)S(1)} collective-permute-done((bf16[2,128,512]{2,1,0:T(8,128)(2,1)}, bf16[2,128,512]{2,1,0:T(8,128)(2,1)S(1)}, u32[]{:S(2)}, u32[]{:S(2)}) %collective-permute-start.16) | collective-permute-done | bytes 262176 | tf_op jit(solution)/shard_map/ppermute | solution.py:338
  140.2 1.3 collective-permute-done.15.refs_7_
  141.5 28.0 %grads.1 = (bf16[6,256,1280]{2,1,0:T(8,128)(2,1)}, bf16[32,128,256]{2,1,0:T(8,128)(2,1)}, bf16[8,128,256]{2,1,0:T(8,128)(2,1)}, bf16[8,128,256]{2,1,0:T(8,128)(2...) custom-call(s32[12]{0:T(128)} %get-tuple-element.19.slot_ref, s32[1]{0:T(128)} %bitcast.10.here_ref, ...), custom_call_target="tpu_custom_call" | custom-call | flops 10000000000 | bytes 25000000 | tf_op jit(solution)/shard_map/grads/pallas_call | solution.py:177
  169.6 6.9 %all-to-all-start.3 = ((bf16[32,128,256]{2,1,0:T(8,128)(2,1)}), bf16[32,128,256]{2,1,0:T(8,128)(2,1)S(1)}, u32[]{:S(2)}, u32[]{:S(2)}) async-start(bf16[32,128,256]{2,1,0:T(8,128)(2,1)} %get-tuple-element.31), calls=%async_computation.3 | async-start | bytes 4194304 | tf_op jit(solution)/shard_map/all_to_all | solution.py:332
  176.6 1.3 collective-permute-start.25
  178.7 1.8 collective-permute-start.27
  180.7 12.1 %collective-permute-done.25 = bf16[8,128,256]{2,1,0:T(8,128)(2,1)S(1)} collective-permute-done((bf16[8,128,256]{2,1,0:T(8,128)(2,1)}, bf16[8,128,256]{2,1,0:T(8,128)(2,1)S(1)}, u32[]{:S(2)}, u32[]{:S(2)}) %collective-permute-start.25) | collective-permute-done | bytes 524320 | tf_op jit(solution)/shard_map/ppermute | solution.py:335
  192.8 2.3 collective-permute-done.26
  195.0 26.9 %collective-permute-done.27 = bf16[8,128,256]{2,1,0:T(8,128)(2,1)S(1)} collective-permute-done((bf16[8,128,256]{2,1,0:T(8,128)(2,1)S(1)}, bf16[8,128,256]{2,1,0:T(8,128)(2,1)S(1)}, u32[]{:S(2)}, u32[]{:S(2)}) %collective-permute-start.27) | collective-permute-done | bytes 524320 | tf_op jit(solution)/shard_map/ppermute | solution.py:335
  222.9 1.9 collective-permute-start.28
  225.2 4.7 %collective-permute-start.30 = (bf16[2,128,256]{2,1,0:T(8,128)(2,1)S(1)}, bf16[2,128,256]{2,1,0:T(8,128)(2,1)S(1)}, u32[]{:S(2)}, u32[]{:S(2)}) collective-permute-start(bf16[2,128,256]{2,1,0:T(8,128)(2,1)S(1)} %get-tuple-element.49), channel_id=1, source_target_pairs={{0,12},{1,13},{2,14},{3,15},{4,16},{5,17},{6,18},{7,19},{8,20},{9,... | collective-permute-start | bytes 393224 | tf_op jit(solution)/shard_map/ppermute | solution.py:338
  230.8 3.8 %collective-permute-start.32 = (bf16[2,128,256]{2,1,0:T(8,128)(2,1)S(1)}, bf16[2,128,256]{2,1,0:T(8,128)(2,1)S(1)}, u32[]{:S(2)}, u32[]{:S(2)}) collective-permute-start(bf16[2,128,256]{2,1,0:T(8,128)(2,1)S(1)} %get-tuple-element.51), channel_id=1, source_target_pairs={{0,20},{1,21},{2,22},{3,23},{4,24},{5,25},{6,26},{7,27},{8,28},{9,... | collective-permute-start | bytes 393224 | tf_op jit(solution)/shard_map/ppermute | solution.py:338
  234.6 1.0 collective-permute-start.34
  235.6 3.6 %collective-permute-start.33 = (bf16[2,128,256]{2,1,0:T(8,128)(2,1)S(1)}, bf16[2,128,256]{2,1,0:T(8,128)(2,1)S(1)}, u32[]{:S(2)}, u32[]{:S(2)}) collective-permute-start(bf16[2,128,256]{2,1,0:T(8,128)(2,1)S(1)} %get-tuple-element.53), channel_id=1, source_target_pairs={{0,24},{1,25},{2,26},{3,27},{4,28},{5,29},{6,30},{7,31},{8,0},{9,1... | collective-permute-start | bytes 393224 | tf_op jit(solution)/shard_map/ppermute | solution.py:338
  239.2 13.7 %query_grad.1 = bf16[240,4096]{1,0:T(8,128)(2,1)} custom-call(s32[12]{0:T(128)} %get-tuple-element.19.slot_ref, s32[1]{0:T(128)} %bitcast.10.here_ref, bf16[6,256,1280]{2,1,0:T(8,128)(2,1)} %get-tuple-element.24.ds_ref, bf16[32,128,512]{2,1,0:T(8,128)(2,1)} %all-to-all-done.2.arrived, bf16[4,128,512]{2,1,0:T(8,128)(2,1)} %copy-done, ...), custom_call_target="tpu_custom_call" | custom-call | flops 3000000000 | bytes 12000000 | tf_op jit(solution)/shard_map/query_grad/pallas_call | solution.py:256
  252.9 6.1 %collective-permute-done.33 = bf16[2,128,256]{2,1,0:T(8,128)(2,1)S(1)} collective-permute-done((bf16[2,128,256]{2,1,0:T(8,128)(2,1)S(1)}, bf16[2,128,256]{2,1,0:T(8,128)(2,1)S(1)}, u32[]{:S(2)}, u32[]{:S(2)}) %collective-permute-start.33) | collective-permute-done | bytes 131104 | tf_op jit(solution)/shard_map/ppermute | solution.py:338
  259.2 1.3 fusion
  (124 shorter events, 19.0 us)
Async XLA Ops:
  3.8 17.4 %all-to-all-start = ((bf16[4,2,128,512]{3,2,1,0:T(8,128)(2,1)}), bf16[4,2,128,512]{3,2,1,0:T(8,128)(2,1)S(1)}, u32[]{:S(2)}, u32[]{:S(2)}) async-start(bf16[4,2,128,512]{3,2,1,0:T(8,128)(2,1)} %broadcast_in_dim.72), calls=%async_computation | async-start | bytes 2097152 | tf_op jit(solution)/shard_map/all_to_all | solution.py:332
  8.0 10.0 %collective-permute-start.2 = (bf16[2,128,512]{2,1,0:T(8,128)(2,1)S(1)}, bf16[2,128,512]{2,1,0:T(8,128)(2,1)S(1)}, u32[]{:S(2)}, u32[]{:S(2)}) collective-permute-start(bf16[2,128,512]{2,1,0:T(8,128)(2,1)S(1)} %bitcast.92), channel_id=1, source_target_pairs={{0,28},{1,29},{2,30},{3,31},{4,0},{5,1},{6,2},{7,3},{8,4},{9,5},{1... | collective-permute-start | bytes 786440 | tf_op jit(solution)/shard_map/ppermute | solution.py:338
  13.6 7.6 %collective-permute-start.1 = (bf16[2,128,512]{2,1,0:T(8,128)(2,1)S(1)}, bf16[2,128,512]{2,1,0:T(8,128)(2,1)S(1)}, u32[]{:S(2)}, u32[]{:S(2)}) collective-permute-start(bf16[2,128,512]{2,1,0:T(8,128)(2,1)S(1)} %bitcast.93), channel_id=1, source_target_pairs={{0,4},{1,5},{2,6},{3,7},{4,8},{5,9},{6,10},{7,11},{8,12},{9,13},{1... | collective-permute-start | bytes 786440 | tf_op jit(solution)/shard_map/ppermute | solution.py:338
  18.0 34.3 %copy-start.12 = (bf16[2,128,512]{2,1,0:T(8,128)(2,1)}, bf16[2,128,512]{2,1,0:T(8,128)(2,1)S(1)}, u32[]{:S(2)}) copy-start(bf16[2,128,512]{2,1,0:T(8,128)(2,1)S(1)} %collective-permute-done.2.refs_7_) | copy-start | bytes 786436
  21.2 31.2 %copy-start.13 = (bf16[2,128,512]{2,1,0:T(8,128)(2,1)}, bf16[2,128,512]{2,1,0:T(8,128)(2,1)S(1)}, u32[]{:S(2)}) copy-start(bf16[2,128,512]{2,1,0:T(8,128)(2,1)S(1)} %collective-permute-done.1.refs_1_) | copy-start | bytes 786436
  21.2 10.4 %collective-permute-start.3 = (bf16[2,128,512]{2,1,0:T(8,128)(2,1)S(1)}, bf16[2,128,512]{2,1,0:T(8,128)(2,1)S(1)}, u32[]{:S(2)}, u32[]{:S(2)}) collective-permute-start(bf16[2,128,512]{2,1,0:T(8,128)(2,1)S(1)} %collective-permute-done.1.refs_1_), channel_id=1, source_target_pairs={{0,4},{1,5},{2,6},{3,7},{4,8},{5,9},{6,10},{7,11},{8,12},{9,13},{1... | collective-permute-start | bytes 786440 | tf_op jit(solution)/shard_map/ppermute | solution.py:338
  22.7 8.8 %collective-permute-start.6 = (bf16[2,128,512]{2,1,0:T(8,128)(2,1)S(1)}, bf16[2,128,512]{2,1,0:T(8,128)(2,1)S(1)}, u32[]{:S(2)}, u32[]{:S(2)}) collective-permute-start(bf16[2,128,512]{2,1,0:T(8,128)(2,1)S(1)} %collective-permute-done.2.refs_7_), channel_id=1, source_target_pairs={{0,28},{1,29},{2,30},{3,31},{4,0},{5,1},{6,2},{7,3},{8,4},{9,5},{1... | collective-permute-start | bytes 786440 | tf_op jit(solution)/shard_map/ppermute | solution.py:338
  26.8 81.7 %copy-start.16 = (s32[12]{0:T(128)}, s32[12]{0:T(128)S(1)}, u32[]{:S(2)}) copy-start(s32[12]{0:T(128)S(1)} %reshape_squeeze.3.dense_slot) | copy-start | bytes 148
  31.5 10.5 %collective-permute-start.4 = (bf16[2,128,512]{2,1,0:T(8,128)(2,1)S(1)}, bf16[2,128,512]{2,1,0:T(8,128)(2,1)S(1)}, u32[]{:S(2)}, u32[]{:S(2)}) collective-permute-start(bf16[2,128,512]{2,1,0:T(8,128)(2,1)S(1)} %collective-permute-done.3.refs_2_), channel_id=1, source_target_pairs={{0,4},{1,5},{2,6},{3,7},{4,8},{5,9},{6,10},{7,11},{8,12},{9,13},{1... | collective-permute-start | bytes 786440 | tf_op jit(solution)/shard_map/ppermute | solution.py:338
  31.6 11.7 %collective-permute-start.7 = (bf16[2,128,512]{2,1,0:T(8,128)(2,1)S(1)}, bf16[2,128,512]{2,1,0:T(8,128)(2,1)S(1)}, u32[]{:S(2)}, u32[]{:S(2)}) collective-permute-start(bf16[2,128,512]{2,1,0:T(8,128)(2,1)S(1)} %collective-permute-done.6.refs_6_), channel_id=1, source_target_pairs={{0,28},{1,29},{2,30},{3,31},{4,0},{5,1},{6,2},{7,3},{8,4},{9,5},{1... | collective-permute-start | bytes 786440 | tf_op jit(solution)/shard_map/ppermute | solution.py:338
  35.0 14.7 %all-to-all-start.1 = ((s32[32,1,8]{2,1,0:T(1,128)}), s32[32,1,8]{2,1,0:T(1,128)S(1)}, u32[]{:S(2)}, u32[]{:S(2)}) async-start(s32[32,1,8]{2,1,0:T(1,128)} %bitcast.5), calls=%async_computation.1 | async-start | bytes 32768 | tf_op jit(solution)/shard_map/all_to_all | solution.py:332
  42.0 9.6 %collective-permute-start.5 = (bf16[1,128,512]{2,1,0:T(8,128)(2,1)S(1)}, bf16[1,128,512]{2,1,0:T(8,128)(2,1)S(1)}, u32[]{:S(2)}, u32[]{:S(2)}) collective-permute-start(bf16[1,128,512]{2,1,0:T(8,128)(2,1)S(1)} %slice.68), channel_id=1, source_target_pairs={{0,4},{1,5},{2,6},{3,7},{4,8},{5,9},{6,10},{7,11},{8,12},{9,13},{1... | collective-permute-start | bytes 393224 | tf_op jit(solution)/shard_map/ppermute | solution.py:338
  43.3 8.3 %collective-permute-start.8 = (bf16[1,128,512]{2,1,0:T(8,128)(2,1)S(1)}, bf16[1,128,512]{2,1,0:T(8,128)(2,1)S(1)}, u32[]{:S(2)}, u32[]{:S(2)}) collective-permute-start(bf16[1,128,512]{2,1,0:T(8,128)(2,1)S(1)} %slice.69), channel_id=1, source_target_pairs={{0,28},{1,29},{2,30},{3,31},{4,0},{5,1},{6,2},{7,3},{8,4},{9,5},{1... | collective-permute-start | bytes 393224 | tf_op jit(solution)/shard_map/ppermute | solution.py:338
  57.8 83.7 %all-to-all-start.2 = ((bf16[32,128,512]{2,1,0:T(8,128)(2,1)}), bf16[32,128,512]{2,1,0:T(8,128)(2,1)}, u32[]{:S(2)}, u32[]{:S(2)}) async-start(bf16[32,128,512]{2,1,0:T(8,128)(2,1)} %serve.1), calls=%async_computation.2 | async-start | bytes 8388608 | tf_op jit(solution)/shard_map/all_to_all | solution.py:332
  63.8 77.7 %copy-start = (bf16[4,128,512]{2,1,0:T(8,128)(2,1)}, bf16[4,128,512]{2,1,0:T(8,128)(2,1)S(1)}, u32[]{:S(2)}) copy-start(bf16[4,128,512]{2,1,0:T(8,128)(2,1)S(1)} %get-tuple-element.55.refs_0_) | copy-start | bytes 1572868
  63.8 8.9 %collective-permute-start.18 = (bf16[4,128,512]{2,1,0:T(8,128)(2,1)S(1)}, bf16[4,128,512]{2,1,0:T(8,128)(2,1)S(1)}, u32[]{:S(2)}, u32[]{:S(2)}) collective-permute-start(bf16[4,128,512]{2,1,0:T(8,128)(2,1)S(1)} %get-tuple-element.54.refs_9_), channel_id=1, source_target_pairs={{0,28},{1,29},{2,30},{3,31},{4,0},{5,1},{6,2},{7,3},{8,4},{9,5},{1... | collective-permute-start | bytes 1572872 | tf_op jit(solution)/shard_map/ppermute | solution.py:338
  64.2 11.5 %collective-permute-start.17 = (bf16[4,128,512]{2,1,0:T(8,128)(2,1)S(1)}, bf16[4,128,512]{2,1,0:T(8,128)(2,1)S(1)}, u32[]{:S(2)}, u32[]{:S(2)}) collective-permute-start(bf16[4,128,512]{2,1,0:T(8,128)(2,1)S(1)} %get-tuple-element.54.refs_9_), channel_id=1, source_target_pairs={{0,4},{1,5},{2,6},{3,7},{4,8},{5,9},{6,10},{7,11},{8,12},{9,13},{1... | collective-permute-start | bytes 1572872 | tf_op jit(solution)/shard_map/ppermute | solution.py:338
  65.4 18.6 %collective-permute-start.10 = (bf16[4,128,512]{2,1,0:T(8,128)(2,1)S(1)}, bf16[4,128,512]{2,1,0:T(8,128)(2,1)S(1)}, u32[]{:S(2)}, u32[]{:S(2)}) collective-permute-start(bf16[4,128,512]{2,1,0:T(8,128)(2,1)S(1)} %get-tuple-element.55.refs_0_), channel_id=1, source_target_pairs={{0,28},{1,29},{2,30},{3,31},{4,0},{5,1},{6,2},{7,3},{8,4},{9,5},{1... | collective-permute-start | bytes 1572872 | tf_op jit(solution)/shard_map/ppermute | solution.py:338
  66.9 18.3 %collective-permute-start.9 = (bf16[4,128,512]{2,1,0:T(8,128)(2,1)S(1)}, bf16[4,128,512]{2,1,0:T(8,128)(2,1)S(1)}, u32[]{:S(2)}, u32[]{:S(2)}) collective-permute-start(bf16[4,128,512]{2,1,0:T(8,128)(2,1)S(1)} %get-tuple-element.55.refs_0_), channel_id=1, source_target_pairs={{0,4},{1,5},{2,6},{3,7},{4,8},{5,9},{6,10},{7,11},{8,12},{9,13},{1... | collective-permute-start | bytes 1572872 | tf_op jit(solution)/shard_map/ppermute | solution.py:338
  66.9 66.6 %collective-permute-start = (bf16[1,240,4096]{2,1,0:T(8,128)(2,1)}, bf16[1,240,4096]{2,1,0:T(8,128)(2,1)}, u32[]{:S(2)}, u32[]{:S(2)}) collective-permute-start(bf16[1,240,4096]{2,1,0:T(8,128)(2,1)} %param.8), channel_id=1, source_target_pairs={{0,224},{32,0},{64,32},{96,64},{128,96},{160,128},{192,160},{224,1... | collective-permute-start | bytes 5898248 | tf_op jit(solution)/shard_map/ppermute | solution.py:375
  72.7 22.5 %collective-permute-start.20 = (bf16[4,128,512]{2,1,0:T(8,128)(2,1)S(1)}, bf16[4,128,512]{2,1,0:T(8,128)(2,1)}, u32[]{:S(2)}, u32[]{:S(2)}) collective-permute-start(bf16[4,128,512]{2,1,0:T(8,128)(2,1)S(1)} %collective-permute-done.18.refs_11_), channel_id=1, source_target_pairs={{0,28},{1,29},{2,30},{3,31},{4,0},{5,1},{6,2},{7,3},{8,4},{9,5},{1... | collective-permute-start | bytes 1572872 | tf_op jit(solution)/shard_map/ppermute | solution.py:338
  75.7 31.9 %copy-start.20 = (bf16[4,128,512]{2,1,0:T(8,128)(2,1)}, bf16[4,128,512]{2,1,0:T(8,128)(2,1)S(1)}, u32[]{:S(2)}) copy-start(bf16[4,128,512]{2,1,0:T(8,128)(2,1)S(1)} %collective-permute-done.17.refs_10_) | copy-start | bytes 1572868
  75.7 20.8 %collective-permute-start.19 = (bf16[4,128,512]{2,1,0:T(8,128)(2,1)S(1)}, bf16[4,128,512]{2,1,0:T(8,128)(2,1)}, u32[]{:S(2)}, u32[]{:S(2)}) collective-permute-start(bf16[4,128,512]{2,1,0:T(8,128)(2,1)S(1)} %collective-permute-done.17.refs_10_), channel_id=1, source_target_pairs={{0,4},{1,5},{2,6},{3,7},{4,8},{5,9},{6,10},{7,11},{8,12},{9,13},{1... | collective-permute-start | bytes 1572872 | tf_op jit(solution)/shard_map/ppermute | solution.py:338
  84.0 57.5 %copy-start.5 = (bf16[4,128,512]{2,1,0:T(8,128)(2,1)}, bf16[4,128,512]{2,1,0:T(8,128)(2,1)S(1)}, u32[]{:S(2)}) copy-start(bf16[4,128,512]{2,1,0:T(8,128)(2,1)S(1)} %collective-permute-done.10.refs_2_) | copy-start | bytes 1572868
  84.0 22.5 %collective-permute-start.12 = (bf16[4,128,512]{2,1,0:T(8,128)(2,1)S(1)}, bf16[4,128,512]{2,1,0:T(8,128)(2,1)S(1)}, u32[]{:S(2)}, u32[]{:S(2)}) collective-permute-start(bf16[4,128,512]{2,1,0:T(8,128)(2,1)S(1)} %collective-permute-done.10.refs_2_), channel_id=1, source_target_pairs={{0,28},{1,29},{2,30},{3,31},{4,0},{5,1},{6,2},{7,3},{8,4},{9,5},{1... | collective-permute-start | bytes 1572872 | tf_op jit(solution)/shard_map/ppermute | solution.py:338
  85.1 56.4 %copy-start.6 = (bf16[4,128,512]{2,1,0:T(8,128)(2,1)}, bf16[4,128,512]{2,1,0:T(8,128)(2,1)S(1)}, u32[]{:S(2)}) copy-start(bf16[4,128,512]{2,1,0:T(8,128)(2,1)S(1)} %collective-permute-done.9.refs_1_) | copy-start | bytes 1572868
  85.1 22.5 %collective-permute-start.11 = (bf16[4,128,512]{2,1,0:T(8,128)(2,1)S(1)}, bf16[4,128,512]{2,1,0:T(8,128)(2,1)}, u32[]{:S(2)}, u32[]{:S(2)}) collective-permute-start(bf16[4,128,512]{2,1,0:T(8,128)(2,1)S(1)} %collective-permute-done.9.refs_1_), channel_id=1, source_target_pairs={{0,4},{1,5},{2,6},{3,7},{4,8},{5,9},{6,10},{7,11},{8,12},{9,13},{1... | collective-permute-start | bytes 1572872 | tf_op jit(solution)/shard_map/ppermute | solution.py:338
  95.2 22.5 %collective-permute-start.22 = (bf16[4,128,512]{2,1,0:T(8,128)(2,1)}, bf16[4,128,512]{2,1,0:T(8,128)(2,1)}, u32[]{:S(2)}, u32[]{:S(2)}) collective-permute-start(bf16[4,128,512]{2,1,0:T(8,128)(2,1)} %collective-permute-done.20.refs_13_), channel_id=1, source_target_pairs={{0,28},{1,29},{2,30},{3,31},{4,0},{5,1},{6,2},{7,3},{8,4},{9,5},{1... | collective-permute-start | bytes 1572872 | tf_op jit(solution)/shard_map/ppermute | solution.py:338
  96.5 24.1 %collective-permute-start.21 = (bf16[4,128,512]{2,1,0:T(8,128)(2,1)}, bf16[4,128,512]{2,1,0:T(8,128)(2,1)}, u32[]{:S(2)}, u32[]{:S(2)}) collective-permute-start(bf16[4,128,512]{2,1,0:T(8,128)(2,1)} %collective-permute-done.19.refs_12_), channel_id=1, source_target_pairs={{0,4},{1,5},{2,6},{3,7},{4,8},{5,9},{6,10},{7,11},{8,12},{9,13},{1... | collective-permute-start | bytes 1572872 | tf_op jit(solution)/shard_map/ppermute | solution.py:338
  106.5 35.1 %copy-start.7 = (bf16[4,128,512]{2,1,0:T(8,128)(2,1)}, bf16[4,128,512]{2,1,0:T(8,128)(2,1)S(1)}, u32[]{:S(2)}) copy-start(bf16[4,128,512]{2,1,0:T(8,128)(2,1)S(1)} %collective-permute-done.12.refs_4_) | copy-start | bytes 1572868
  106.5 22.5 %collective-permute-start.14 = (bf16[4,128,512]{2,1,0:T(8,128)(2,1)S(1)}, bf16[4,128,512]{2,1,0:T(8,128)(2,1)S(1)}, u32[]{:S(2)}, u32[]{:S(2)}) collective-permute-start(bf16[4,128,512]{2,1,0:T(8,128)(2,1)S(1)} %collective-permute-done.12.refs_4_), channel_id=1, source_target_pairs={{0,28},{1,29},{2,30},{3,31},{4,0},{5,1},{6,2},{7,3},{8,4},{9,5},{1... | collective-permute-start | bytes 1572872 | tf_op jit(solution)/shard_map/ppermute | solution.py:338
  107.6 23.2 %collective-permute-start.13 = (bf16[4,128,512]{2,1,0:T(8,128)(2,1)}, bf16[4,128,512]{2,1,0:T(8,128)(2,1)S(1)}, u32[]{:S(2)}, u32[]{:S(2)}) collective-permute-start(bf16[4,128,512]{2,1,0:T(8,128)(2,1)} %collective-permute-done.11.refs_3_), channel_id=1, source_target_pairs={{0,4},{1,5},{2,6},{3,7},{4,8},{5,9},{6,10},{7,11},{8,12},{9,13},{1... | collective-permute-start | bytes 1572872 | tf_op jit(solution)/shard_map/ppermute | solution.py:338
  119.4 15.1 %collective-permute-start.24 = (bf16[2,128,512]{2,1,0:T(8,128)(2,1)}, bf16[2,128,512]{2,1,0:T(8,128)(2,1)}, u32[]{:S(2)}, u32[]{:S(2)}) collective-permute-start(bf16[2,128,512]{2,1,0:T(8,128)(2,1)} %slice.75), channel_id=1, source_target_pairs={{0,28},{1,29},{2,30},{3,31},{4,0},{5,1},{6,2},{7,3},{8,4},{9,5},{1... | collective-permute-start | bytes 786440 | tf_op jit(solution)/shard_map/ppermute | solution.py:338
  122.3 13.1 %collective-permute-start.23 = (bf16[2,128,512]{2,1,0:T(8,128)(2,1)}, bf16[2,128,512]{2,1,0:T(8,128)(2,1)}, u32[]{:S(2)}, u32[]{:S(2)}) collective-permute-start(bf16[2,128,512]{2,1,0:T(8,128)(2,1)} %slice.74), channel_id=1, source_target_pairs={{0,4},{1,5},{2,6},{3,7},{4,8},{5,9},{6,10},{7,11},{8,12},{9,13},{1... | collective-permute-start | bytes 786440 | tf_op jit(solution)/shard_map/ppermute | solution.py:338
  129.7 10.5 %collective-permute-start.16 = (bf16[2,128,512]{2,1,0:T(8,128)(2,1)}, bf16[2,128,512]{2,1,0:T(8,128)(2,1)S(1)}, u32[]{:S(2)}, u32[]{:S(2)}) collective-permute-start(bf16[2,128,512]{2,1,0:T(8,128)(2,1)} %slice.72), channel_id=1, source_target_pairs={{0,28},{1,29},{2,30},{3,31},{4,0},{5,1},{6,2},{7,3},{8,4},{9,5},{1... | collective-permute-start | bytes 786440 | tf_op jit(solution)/shard_map/ppermute | solution.py:338
  131.6 9.9 %collective-permute-start.15 = (bf16[2,128,512]{2,1,0:T(8,128)(2,1)}, bf16[2,128,512]{2,1,0:T(8,128)(2,1)}, u32[]{:S(2)}, u32[]{:S(2)}) collective-permute-start(bf16[2,128,512]{2,1,0:T(8,128)(2,1)} %slice.71), channel_id=1, source_target_pairs={{0,4},{1,5},{2,6},{3,7},{4,8},{5,9},{6,10},{7,11},{8,12},{9,13},{1... | collective-permute-start | bytes 786440 | tf_op jit(solution)/shard_map/ppermute | solution.py:338
  169.6 52.4 %copy-start.9 = (bf16[8,128,256]{2,1,0:T(8,128)(2,1)S(1)}, bf16[8,128,256]{2,1,0:T(8,128)(2,1)}, u32[]{:S(2)}) copy-start(bf16[8,128,256]{2,1,0:T(8,128)(2,1)} %get-tuple-element.26) | copy-start | bytes 1572868
  169.6 89.6 %all-to-all-start.3 = ((bf16[32,128,256]{2,1,0:T(8,128)(2,1)}), bf16[32,128,256]{2,1,0:T(8,128)(2,1)S(1)}, u32[]{:S(2)}, u32[]{:S(2)}) async-start(bf16[32,128,256]{2,1,0:T(8,128)(2,1)} %get-tuple-element.31), calls=%async_computation.3 | async-start | bytes 4194304 | tf_op jit(solution)/shard_map/all_to_all | solution.py:332
  176.6 16.2 %collective-permute-start.25 = (bf16[8,128,256]{2,1,0:T(8,128)(2,1)}, bf16[8,128,256]{2,1,0:T(8,128)(2,1)S(1)}, u32[]{:S(2)}, u32[]{:S(2)}) collective-permute-start(bf16[8,128,256]{2,1,0:T(8,128)(2,1)} %get-tuple-element.27), channel_id=1, source_target_pairs={{0,1},{1,2},{2,3},{3,0},{4,5},{5,6},{6,7},{7,4},{8,9},{9,10},{10,1... | collective-permute-start | bytes 1572872 | tf_op jit(solution)/shard_map/ppermute | solution.py:335
  177.8 17.2 %collective-permute-start.26 = (bf16[8,128,256]{2,1,0:T(8,128)(2,1)}, bf16[8,128,256]{2,1,0:T(8,128)(2,1)S(1)}, u32[]{:S(2)}, u32[]{:S(2)}) collective-permute-start(bf16[8,128,256]{2,1,0:T(8,128)(2,1)} %get-tuple-element.28), channel_id=1, source_target_pairs={{0,2},{1,3},{2,0},{3,1},{4,6},{5,7},{6,4},{7,5},{8,10},{9,11},{10,... | collective-permute-start | bytes 1572872 | tf_op jit(solution)/shard_map/ppermute | solution.py:335
  178.7 43.2 %collective-permute-start.27 = (bf16[8,128,256]{2,1,0:T(8,128)(2,1)S(1)}, bf16[8,128,256]{2,1,0:T(8,128)(2,1)S(1)}, u32[]{:S(2)}, u32[]{:S(2)}) collective-permute-start(bf16[8,128,256]{2,1,0:T(8,128)(2,1)S(1)} %copy-done.21), channel_id=1, source_target_pairs={{0,3},{1,0},{2,1},{3,2},{4,7},{5,4},{6,5},{7,6},{8,11},{9,8},{10,9... | collective-permute-start | bytes 1572872 | tf_op jit(solution)/shard_map/ppermute | solution.py:335
  222.9 11.7 %collective-permute-start.28 = (bf16[2,128,256]{2,1,0:T(8,128)(2,1)S(1)}, bf16[2,128,256]{2,1,0:T(8,128)(2,1)S(1)}, u32[]{:S(2)}, u32[]{:S(2)}) collective-permute-start(bf16[2,128,256]{2,1,0:T(8,128)(2,1)S(1)} %get-tuple-element.47), channel_id=1, source_target_pairs={{0,4},{1,5},{2,6},{3,7},{4,8},{5,9},{6,10},{7,11},{8,12},{9,13},{1... | collective-permute-start | bytes 393224 | tf_op jit(solution)/shard_map/ppermute | solution.py:338
  224.8 10.8 %collective-permute-start.29 = (bf16[2,128,256]{2,1,0:T(8,128)(2,1)S(1)}, bf16[2,128,256]{2,1,0:T(8,128)(2,1)S(1)}, u32[]{:S(2)}, u32[]{:S(2)}) collective-permute-start(bf16[2,128,256]{2,1,0:T(8,128)(2,1)S(1)} %get-tuple-element.48), channel_id=1, source_target_pairs={{0,8},{1,9},{2,10},{3,11},{4,12},{5,13},{6,14},{7,15},{8,16},{9,17... | collective-permute-start | bytes 393224 | tf_op jit(solution)/shard_map/ppermute | solution.py:338
  225.2 27.7 %collective-permute-start.30 = (bf16[2,128,256]{2,1,0:T(8,128)(2,1)S(1)}, bf16[2,128,256]{2,1,0:T(8,128)(2,1)S(1)}, u32[]{:S(2)}, u32[]{:S(2)}) collective-permute-start(bf16[2,128,256]{2,1,0:T(8,128)(2,1)S(1)} %get-tuple-element.49), channel_id=1, source_target_pairs={{0,12},{1,13},{2,14},{3,15},{4,16},{5,17},{6,18},{7,19},{8,20},{9,... | collective-permute-start | bytes 393224 | tf_op jit(solution)/shard_map/ppermute | solution.py:338
  230.0 22.9 %collective-permute-start.31 = (bf16[2,128,256]{2,1,0:T(8,128)(2,1)S(1)}, bf16[2,128,256]{2,1,0:T(8,128)(2,1)S(1)}, u32[]{:S(2)}, u32[]{:S(2)}) collective-permute-start(bf16[2,128,256]{2,1,0:T(8,128)(2,1)S(1)} %get-tuple-element.50), channel_id=1, source_target_pairs={{0,16},{1,17},{2,18},{3,19},{4,20},{5,21},{6,22},{7,23},{8,24},{9,... | collective-permute-start | bytes 393224 | tf_op jit(solution)/shard_map/ppermute | solution.py:338
  230.8 22.1 %collective-permute-start.32 = (bf16[2,128,256]{2,1,0:T(8,128)(2,1)S(1)}, bf16[2,128,256]{2,1,0:T(8,128)(2,1)S(1)}, u32[]{:S(2)}, u32[]{:S(2)}) collective-permute-start(bf16[2,128,256]{2,1,0:T(8,128)(2,1)S(1)} %get-tuple-element.51), channel_id=1, source_target_pairs={{0,20},{1,21},{2,22},{3,23},{4,24},{5,25},{6,26},{7,27},{8,28},{9,... | collective-permute-start | bytes 393224 | tf_op jit(solution)/shard_map/ppermute | solution.py:338
  234.6 18.3 %collective-permute-start.34 = (bf16[2,128,256]{2,1,0:T(8,128)(2,1)S(1)}, bf16[2,128,256]{2,1,0:T(8,128)(2,1)S(1)}, u32[]{:S(2)}, u32[]{:S(2)}) collective-permute-start(bf16[2,128,256]{2,1,0:T(8,128)(2,1)S(1)} %get-tuple-element.52), channel_id=1, source_target_pairs={{0,28},{1,29},{2,30},{3,31},{4,0},{5,1},{6,2},{7,3},{8,4},{9,5},{1... | collective-permute-start | bytes 393224 | tf_op jit(solution)/shard_map/ppermute | solution.py:338
  235.6 23.4 %collective-permute-start.33 = (bf16[2,128,256]{2,1,0:T(8,128)(2,1)S(1)}, bf16[2,128,256]{2,1,0:T(8,128)(2,1)S(1)}, u32[]{:S(2)}, u32[]{:S(2)}) collective-permute-start(bf16[2,128,256]{2,1,0:T(8,128)(2,1)S(1)} %get-tuple-element.53), channel_id=1, source_target_pairs={{0,24},{1,25},{2,26},{3,27},{4,28},{5,29},{6,30},{7,31},{8,0},{9,1... | collective-permute-start | bytes 393224 | tf_op jit(solution)/shard_map/ppermute | solution.py:338
  (13 other events, 184.4 us)
